TPU v7x, 32 devices: a whole 2x2x4 slice. The times are simulated.
32 devices in a mesh: groups: 2 (over x), module: 16 (over z, y, core).
Axes of the slice: x: 2, y: 2, z: 4, core: 2. Of those that a mesh axis runs over, the one named last changes fastest.
Arguments:
- act_table: bfloat16 [4096, 1024], P(('groups', 'module')), parts along dimension 0, may hold values from -6 to 6
- grad_table: bfloat16 [4096, 1024], P(('groups', 'module')), parts along dimension 0, may hold values from -6 to 6
- token_rows: int32 [256, 128], P(('groups', 'module')), parts along dimension 0, may hold values from 0 to 127
- left_inv: bfloat16 [16, 64, 64], P('module'), may hold values from -3 to 3.5
- right_inv: bfloat16 [16, 64, 64], P('module'), may hold values from -3 to 3.5
- query_grads: bfloat16 [256, 16, 4096], P('groups', 'module'), parts along dimension 0, may hold values from -0.03125 to 0.03125
Outputs:
- scores: float32 [256, 128], P(('groups', 'module')), parts along dimension 0
There are 2 independent parts, one for each index of `groups`. A program takes and returns all parts, laid end to end along the dimension named above; an argument that names none is the same for every part. Nothing has to cross between parts.
Inputs may be any that keep to these rules, and one draw needn't show every extreme that they name: `token_rows`: each example's rows index the 128 table rows held with its block of 8 examples (the block's token states are stored deduplicated, so tokens of the block share these rows).
All inputs are finite; a program needn't handle non-finite values.
Results may differ from a plain program's by a relative error of at most 0.0049.
Values may be sent and summed in bfloat16 or wider, within the bound.
No kernel may reach another device: no remote copies, remote signals or barrier semaphores. Data moves between devices by JAX's collectives and lax.ppermute only.
A program may use at most 128 MiB of HBM per device.

v0:
```python
import math

import jax
import jax.numpy as jnp
from jax import lax
from jax.sharding import PartitionSpec as P


def apply_factors(blocks_in, left_part, right_part):
    middle = jnp.einsum(
        "emjk,mkl->emjl", blocks_in, right_part, preferred_element_type=jnp.float32
    ).astype(jnp.bfloat16)
    return jnp.einsum(
        "mij,emjl->emil", left_part, middle, preferred_element_type=jnp.float32
    ).astype(jnp.bfloat16)


def per_device(act_table, grad_table, token_rows, left_inv, right_inv, query_grads):
    rank_size = left_inv.shape[1]
    local_modules = left_inv.shape[0]
    modules = act_table.shape[1] // rank_size
    examples, tokens = token_rows.shape
    act_rows = act_table[token_rows].reshape(examples, tokens, modules, rank_size)
    grad_rows = grad_table[token_rows].reshape(examples, tokens, modules, rank_size)
    outer_sum = jnp.einsum(
        "etmi,etmj->emij", grad_rows, act_rows, preferred_element_type=jnp.float32
    ) / math.sqrt(tokens)
    per_example = outer_sum.astype(jnp.bfloat16)
    shipped = per_example
    shipped = shipped.reshape(examples, modules, rank_size * rank_size)
    regrouped = lax.all_to_all(shipped, "module", split_axis=1, concat_axis=0, tiled=True)
    row_total = regrouped.shape[0]
    squared = regrouped.reshape(row_total, local_modules, rank_size, rank_size)
    conditioned = apply_factors(squared, left_inv, right_inv)
    prepared = conditioned.reshape(row_total, local_modules, rank_size * rank_size)
    return lax.psum_scatter(
        jnp.einsum("qmf,emf->qe", query_grads, prepared, preferred_element_type=jnp.float32),
        "module",
        scatter_dimension=0,
        tiled=True,
    )


def solution(mesh):
    placed = (
        P(("groups", "module"), None),
        P(("groups", "module"), None),
        P(("groups", "module"), None),
        P("module", None, None),
        P("module", None, None),
        P("groups", "module", None),
    )
    return jax.shard_map(
        per_device,
        mesh=mesh,
        in_specs=placed,
        out_specs=P(("groups", "module"), None),
        check_vma=False,
    )
```

profile of v0, /device:TPU:0, one launch (start us, length us, event | category | flops | bytes accessed | tf_op | source)
XLA Modules:
  0.0 175.2 jit_solution(10843797104215887508)
XLA Ops:
  6.5 0.0 copy-start
  6.5 0.0 all-reduce.3.cloned.1.call-start
  6.5 0.8 fusion.12
  7.3 6.0 %gather_fusion = bf16[1024,1024]{1,0:T(8,128)(2,1)S(1)} fusion(bf16[128,1024]{1,0:T(8,128)(2,1)} %param.7, s32[1024]{0:T(1024)S(1)} %fusion.12), kind=kCustom, calls=%fused_computation | custom fusion | bytes 4198400 | tf_op jit(solution)/shard_map/gather | solution.py:24
  13.3 0.0 copy-start.1
  13.3 4.0 %reshape.66 = bf16[8,128,16,64]{3,2,1,0:T(8,128)(2,1)} reshape(bf16[1024,1024]{1,0:T(8,128)(2,1)S(1)} %gather_fusion) | data formatting | bytes 4194304 | tf_op jit(solution)/shard_map/reshape | solution.py:24
  17.3 0.0 copy-done.1
  17.3 4.1 %gather_fusion.1 = bf16[1024,1024]{1,0:T(8,128)(2,1)S(1)} fusion(bf16[128,1024]{1,0:T(8,128)(2,1)S(1)} %copy-done.1, s32[1024]{0:T(1024)S(1)} %fusion.12), kind=kCustom, calls=%fused_computation.1 | custom fusion | bytes 4198400 | tf_op jit(solution)/shard_map/gather | solution.py:23
  21.4 4.0 %reshape.67 = bf16[8,128,16,64]{3,2,1,0:T(8,128)(2,1)} reshape(bf16[1024,1024]{1,0:T(8,128)(2,1)S(1)} %gather_fusion.1) | data formatting | bytes 4194304 | tf_op jit(solution)/shard_map/reshape | solution.py:23
  25.4 6.6 %multiply_convert_fusion = bf16[8,16,64,64]{3,2,1,0:T(8,128)(2,1)} fusion(bf16[8,128,16,64]{3,2,1,0:T(8,128)(2,1)} %reshape.67, bf16[8,128,16,64]{3,2,1,0:T(8,128)(2,1)} %reshape.66), kind=kOutput, calls=%fused_computation.5 | convolution fusion | flops 135266304 | bytes 5242880 | tf_op jit(solution)/shard_map/etmi,etmj->emij/dot_general | solution.py:25
  32.0 3.3 %reshape.36 = bf16[8,16,4096]{2,1,0:T(8,128)(2,1)S(1)} reshape(bf16[8,16,64,64]{3,2,1,0:T(8,128)(2,1)} %multiply_convert_fusion) | data formatting | bytes 2097152 | tf_op jit(solution)/shard_map/reshape | solution.py:30
  35.3 0.6 copy.21
  35.9 32.0 %all_to_all.15 = bf16[8,16,4096]{2,0,1:T(8,128)(2,1)} all-to-all(bf16[8,16,4096]{2,0,1:T(8,128)(2,1)S(1)} %copy.21), channel_id=1, replica_groups=mesh['groups'=2,'module'=16] {'module'}, dimensions={1} | all-to-all | bytes 2097152 | tf_op jit(solution)/shard_map/all_to_all | solution.py:31
  67.9 0.0 copy-start.2
  67.9 3.3 %reshape.37 = bf16[128,64,64]{2,1,0:T(8,128)(2,1)S(1)} reshape(bf16[16,8,1,4096]{3,1,0,2:T(8,128)(2,1)} %bitcast.37) | data formatting | bytes 2097152 | tf_op jit(solution)/shard_map/reshape.2
  71.2 0.0 copy-done.2
  71.2 2.0 %convolution_convert_fusion = bf16[128,64,64]{2,1,0:T(8,128)(2,1)} fusion(bf16[128,64,64]{2,1,0:T(8,128)(2,1)S(1)} %reshape.37, bf16[1,64,64]{2,1,0:T(8,128)(2,1)S(1)} %copy-done.2), kind=kOutput, calls=%fused_computation.6 | convolution fusion | flops 67633152 | bytes 2105344 | tf_op jit(solution)/shard_map/emjk,mkl->emjl/dot_general | solution.py:10
  73.2 0.0 copy-start.3
  73.2 4.5 %copy.22 = bf16[128,64,64]{0,1,2:T(8,128)(2,1)S(1)} copy(bf16[128,64,64]{2,1,0:T(8,128)(2,1)} %convolution_convert_fusion) | data formatting | bytes 2097152 | tf_op jit(solution)/shard_map/convert_element_type | solution.py:12
  77.7 0.0 copy-done.3
  77.7 0.4 fusion.7
  78.1 0.0 copy-start.4
  78.2 0.7 copy.23
  78.8 0.0 copy-done
  78.9 1.1 convolution_bitcast_fusion
  79.9 0.0 all-reduce.3.cloned.1.call-update
  80.0 0.0 copy-done.4
  80.0 0.6 dynamic-slice
  81.2 85.5 %all-reduce.3.cloned.1.call-done = f32[128,128]{0,1:T(8,128)} async-done(((f32[128,128]{0,1:T(8,128)}), f32[128,128]{0,1:T(8,128)}) %all-reduce.3.cloned.1.call-update) | async-done | bytes 65552
  166.8 0.9 constant_dynamic-slice_fusion
  167.7 0.7 copy.24
Async XLA Ops:
  6.5 72.3 %copy-start = (bf16[128,1,4096]{2,0,1:T(8,128)(2,1)S(1)}, bf16[128,1,4096]{2,0,1:T(8,128)(2,1)}, u32[]{:S(2)}) copy-start(bf16[128,1,4096]{2,0,1:T(8,128)(2,1)} %param.11) | copy-start | bytes 3145732
  6.5 160.2 %all-reduce.3.cloned.1.call-start = ((), (), s32[]{:S(2)}) async-start(), calls=%async_computation.1 | async-start | bytes 131072
  13.3 4.0 %copy-start.1 = (bf16[128,1024]{1,0:T(8,128)(2,1)S(1)}, bf16[128,1024]{1,0:T(8,128)(2,1)}, u32[]{:S(2)}) copy-start(bf16[128,1024]{1,0:T(8,128)(2,1)} %param.6) | copy-start | bytes 786436
  67.9 3.3 %copy-start.2 = (bf16[1,64,64]{2,1,0:T(8,128)(2,1)S(1)}, bf16[1,64,64]{2,1,0:T(8,128)(2,1)}, u32[]{:S(2)}) copy-start(bf16[1,64,64]{2,1,0:T(8,128)(2,1)} %param.10) | copy-start | bytes 24580
  73.2 4.5 %copy-start.3 = (bf16[1,64,64]{2,1,0:T(8,128)(2,1)S(1)}, bf16[1,64,64]{2,1,0:T(8,128)(2,1)}, u32[]{:S(2)}) copy-start(bf16[1,64,64]{2,1,0:T(8,128)(2,1)} %param.9) | copy-start | bytes 24580
  78.1 1.8 %copy-start.4 = (u32[32]{0:T(128)S(1)}, u32[32]{0:T(128)}, u32[]{:S(2)}) copy-start(u32[32]{0:T(128)} %constant.13) | copy-start | bytes 388
Sparse Core Ops, SparseCore 0:
  80.1 86.6 all-reduce.2
where the time goes:
time: 177 us; the launch traced here: 175 us
  waiting for transfers between devices  85.6 us (48%)
  local copies, waits for them, and re-layouts  32.6 us (18%)
  blocking collectives  32 us (18%)
  between operations  14.2 us (8%)
  matrix products  10.1 us (6%)
    unnamed x2, waiting for transfers between devices  85.6 us
    all_to_all x1, blocking collectives, per_device(): lax.all_to_all(shipped, 'module', split_axis=1, concat_axis=0, tiled=True)  32 us
    dot_general x1, matrix products, per_device(): jnp.einsum('etmi,etmj->emij', grad_rows, act_rows, preferred_element_type...  6.58 us
    gather x1, local copies, waits for them, and re-layouts, per_device(): grad_table[token_rows].reshape(examples, tokens, modules, rank_size)  5.96 us
    convert_element_type x1, local copies, waits for them, and re-layouts, apply_factors(): middle = jnp.einsum('emjk,mkl->emjl', blocks_in, right_part, preferred_el...  4.52 us
    gather x1, local copies, waits for them, and re-layouts, per_device(): act_table[token_rows].reshape(examples, tokens, modules, rank_size)  4.06 us
    reshape x1, local copies, waits for them, and re-layouts, per_device(): grad_table[token_rows].reshape(examples, tokens, modules, rank_size)  4.01 us
    reshape x1, local copies, waits for them, and re-layouts, per_device(): act_table[token_rows].reshape(examples, tokens, modules, rank_size)  4 us
  transfers between devices with their start and end apart: 1, of which 1 were waited for; matrix products, arithmetic and copies ran while one was open for 0% of the time, Pallas kernels for 0%

commit v1 on v0

v1 whole, which is shorter than its diff:
```python
import functools
import math

import jax
import jax.numpy as jnp
from jax import lax
from jax.experimental import pallas as pl
from jax.experimental.pallas import tpu as pltpu
from jax.sharding import PartitionSpec as P


def pack_kernel(act_ref, grad_ref, tok_ref, out_ref):
    owners = out_ref.shape[0]
    rows = act_ref.shape[0]
    rank = act_ref.shape[1] // owners
    examples, tokens = tok_ref.shape
    for owner in range(owners):
        columns = slice(owner * rank, (owner + 1) * rank)
        out_ref[owner, :rows, :] = jnp.concatenate([grad_ref[:, columns], act_ref[:, columns]], axis=1)
    tok = tok_ref[...]
    row_of_lane = lax.broadcasted_iota(jnp.int32, (examples, rows), 1)
    counts = jnp.zeros((examples, rows), jnp.float32)
    for t in range(tokens):
        counts += jnp.where(tok[:, t : t + 1] == row_of_lane, 1.0, 0.0)
    counts = counts.astype(jnp.bfloat16)
    for owner in range(owners):
        out_ref[owner, rows:, :] = counts


def owner_kernel(scale, recv_hbm, query_hbm, left_ref, right_ref, out_ref, recv, query, spread, grads, cond, recv_sem, query_sem):
    blocks, height, width = recv.shape
    rank = left_ref.shape[-1]
    rows = width
    examples = height - rows
    half = rank // 2
    arrivals = [pltpu.make_async_copy(recv_hbm.at[b], recv.at[b], recv_sem.at[b]) for b in range(blocks)]
    for copy in arrivals:
        copy.start()
    query_copy = pltpu.make_async_copy(query_hbm, query, query_sem)
    query_copy.start()

    left = left_ref[0]
    right = right_ref[0]
    spread[...] = jnp.zeros_like(spread)
    spread[rank:, :rank] = right
    spread[rank:, 3 * rank :] = right

    def one(b):
        table = recv[b, :rows, :]
        counts = recv[b, rows:, :].astype(jnp.float32)
        slot = b % grads.shape[0]
        grads[slot] = lax.dot_general(left, table[:, :rank], (((1,), (1,)), ((), ())), preferred_element_type=jnp.float32)
        acts = jnp.dot(table, spread[...], preferred_element_type=jnp.float32)
        high = acts.astype(jnp.bfloat16)
        low = (acts - high.astype(jnp.float32)).astype(jnp.bfloat16)
        weights = jnp.concatenate(
            [
                jnp.concatenate([high[:, :width], low[:, :width]], axis=1),
                jnp.concatenate([high[:, width:], low[:, width:]], axis=1),
            ],
            axis=0,
        )
        columns = []
        for parity in range(2):
            pieces = [grads[slot, pl.ds(2 * p + parity, 1), :] * counts for p in range(half)]
            columns.append(jnp.concatenate(pieces, axis=0).astype(jnp.bfloat16))
        weighted = jnp.concatenate(columns, axis=1)
        product = jnp.dot(weighted, weights, preferred_element_type=jnp.float32)
        return product[:, :width] + product[:, width:]

    for b in range(0, blocks, 2):
        arrivals[b].wait()
        arrivals[b + 1].wait()
        first, second = one(b), one(b + 1)
        for p in range(half):
            piece = slice(p * examples, (p + 1) * examples)
            cond[b * examples : (b + 2) * examples, p * width : (p + 1) * width] = jnp.concatenate(
                [first[piece], second[piece]], axis=0
            ).astype(jnp.bfloat16)

    query_copy.wait()
    scores = lax.dot_general(query[...], cond[...], (((1,), (1,)), ((), ())), preferred_element_type=jnp.float32)
    out_ref[...] = scores * scale


def per_device(owners, act_table, grad_table, token_rows, left_inv, right_inv, query_grads):
    rows, columns = act_table.shape
    examples, tokens = token_rows.shape
    local_modules, rank, _ = left_inv.shape
    queries = query_grads.shape[0]
    width = 2 * rank
    assert local_modules == 1 and columns == owners * rank
    assert rows == width and tokens <= 256 and examples % 8 == 0
    height = rows + examples

    packed = pl.pallas_call(
        pack_kernel,
        out_shape=jax.ShapeDtypeStruct((owners, height, width), jnp.bfloat16),
        name="pack",
    )(act_table, grad_table, token_rows)
    recv = lax.all_to_all(packed, "module", split_axis=0, concat_axis=0, tiled=True)

    partial = pl.pallas_call(
        functools.partial(owner_kernel, 1.0 / math.sqrt(tokens)),
        out_shape=jax.ShapeDtypeStruct((queries, owners * examples), jnp.float32),
        in_specs=[
            pl.BlockSpec(memory_space=pl.ANY),
            pl.BlockSpec(memory_space=pl.ANY),
            pl.BlockSpec(memory_space=pltpu.VMEM),
            pl.BlockSpec(memory_space=pltpu.VMEM),
        ],
        out_specs=pl.BlockSpec(memory_space=pltpu.VMEM),
        scratch_shapes=[
            pltpu.VMEM((owners, height, width), jnp.bfloat16),
            pltpu.VMEM((queries, rank * rank), jnp.bfloat16),
            pltpu.VMEM((width, 2 * width), jnp.bfloat16),
            pltpu.VMEM((4, rank, rows), jnp.float32),
            pltpu.VMEM((owners * examples, rank * rank), jnp.bfloat16),
            pltpu.SemaphoreType.DMA((owners,)),
            pltpu.SemaphoreType.DMA,
        ],
        name="owner",
    )(recv, query_grads.reshape(queries, rank * rank), left_inv, right_inv)

    tiles = partial.reshape(owners, queries // owners, owners * examples)
    gathered = lax.all_to_all(tiles, "module", split_axis=0, concat_axis=0, tiled=True)
    return jnp.sum(gathered, axis=0)


def solution(mesh):
    placed = (
        P(("groups", "module"), None),
        P(("groups", "module"), None),
        P(("groups", "module"), None),
        P("module", None, None),
        P("module", None, None),
        P("groups", "module", None),
    )
    return jax.shard_map(
        functools.partial(per_device, mesh.shape["module"]),
        mesh=mesh,
        in_specs=placed,
        out_specs=P(("groups", "module"), None),
        check_vma=False,
    )
```

time: 177 us -> 45.2 us (0.26)
  waiting for transfers between devices: 85.6 us -> 0 us
  local copies, waits for them, and re-layouts: 32.6 us -> 0 us
  between operations: 14.2 us -> 0.01 us
  matrix products: 10.1 us -> 0 us
  Pallas kernels: 0 us -> 9.57 us
  blocking collectives: 32 us -> 34.6 us
    unnamed x2 -> x0, waiting for transfers between devices: 85.6 us -> none
    reshape x4 -> x0, local copies, waits for them, and re-layouts: 11.9 us -> none  [the longest x1 4.01 us: per_device(): grad_table[token_rows].reshape(examples, tokens, modules, rank_size)]
    dot_general x4 -> x0, matrix products: 10.1 us -> none  [the longest x1 6.58 us: per_device(): jnp.einsum('etmi,etmj->emij', grad_rows, act_rows, preferred_element_type...]
    gather x2 -> x0, local copies, waits for them, and re-layouts: 10 us -> none  [the longest x1 5.96 us: per_device(): grad_table[token_rows].reshape(examples, tokens, modules, rank_size)]
    pallas_call x0 -> x2, Pallas kernels: none -> 9.57 us  [the longest x1 7.31 us: per_device(): pl.pallas_call(functools.partial(owner_kernel, 1.0 / math.sqrt(tokens)),...]
    convert_element_type x2 -> x0, local copies, waits for them, and re-layouts: 5.2 us -> none  [the longest x1 4.52 us: apply_factors(): middle = jnp.einsum('emjk,mkl->emjl', blocks_in, right_part, preferred_el...]
    another operation x1 -> x0, local copies, waits for them, and re-layouts: 3.27 us -> none
    all_to_all x1 -> x2, blocking collectives: 32 us -> 34.6 us  [the longest x1 24.2 us: per_device(): lax.all_to_all(packed, 'module', split_axis=0, concat_axis=0, tiled=True)]
  transfers between devices with their start and end apart: 1 -> 0, of which waited for: 1 -> 0; matrix products, arithmetic and copies ran while one was open for 0% -> 0% of each run, Pallas kernels for 0% -> 0%
where the time goes in v1:
time: 45.2 us; the launch traced here: 44.7 us
  blocking collectives  34.6 us (77%)
  Pallas kernels  9.57 us (21%)
  other arithmetic  0.61 us (1%)
    all_to_all x1, blocking collectives, per_device(): lax.all_to_all(packed, 'module', split_axis=0, concat_axis=0, tiled=True)  24.2 us
    all_to_all x1, blocking collectives, per_device(): lax.all_to_all(tiles, 'module', split_axis=0, concat_axis=0, tiled=True)  10.4 us
    pallas_call x1, Pallas kernels, per_device(): pl.pallas_call(functools.partial(owner_kernel, 1.0 / math.sqrt(tokens)),...  7.31 us
    pallas_call x1, Pallas kernels, per_device(): pl.pallas_call(pack_kernel, out_shape=jax.ShapeDtypeStruct((owners, heigh...  2.26 us

profile of v1, /device:TPU:0, one launch (start us, length us, event | category | flops | bytes accessed | tf_op | source)
XLA Modules:
  0.0 44.7 jit_solution(6057190240251454203)
XLA Ops:
  0.0 2.3 %pack.1 = bf16[16,136,128]{2,1,0:T(8,128)(2,1)} custom-call(bf16[128,1024]{1,0:T(8,128)(2,1)} %act_ref.1, bf16[128,1024]{1,0:T(8,128)(2,1)} %grad_ref.1, s32[8,128]{1,0:T(8,128)} %tok_ref.1), custom_call_target="tpu_custom_call" | custom-call | tf_op jit(solution)/shard_map/pack/pallas_call | solution.py:96
  2.3 24.2 %all_to_all.10.recv_hbm = bf16[16,136,128]{2,1,0:T(8,128)(2,1)} all-to-all(bf16[16,136,128]{2,1,0:T(8,128)(2,1)} %pack.1), channel_id=1, replica_groups=mesh['groups'=2,'module'=16] {'module'}, dimensions={0} | all-to-all | bytes 1114112 | tf_op jit(solution)/shard_map/all_to_all | solution.py:101
  26.5 7.3 %owner.1 = f32[128,128]{1,0:T(8,128)} custom-call(bf16[16,136,128]{2,1,0:T(8,128)(2,1)} %all_to_all.10.recv_hbm, bf16[128,4096]{1,0:T(8,128)(2,1)} %bitcast.2, bf16[1,64,64]{2,1,0:T(8,128)(2,1)} %left_ref.1, bf16[1,64,64]{2,1,0:T(8,128)(2,1)} %right_ref.1), custom_call_target="tpu_custom_call" | custom-call | tf_op jit(solution)/shard_map/owner/pallas_call | solution.py:103
  33.8 10.4 %all_to_all.11 = f32[16,8,128]{2,1,0:T(8,128)S(1)} all-to-all(f32[16,8,128]{2,1,0:T(8,128)} %bitcast.3), channel_id=1, replica_groups=mesh['groups'=2,'module'=16] {'module'}, dimensions={0} | all-to-all | bytes 131072 | tf_op jit(solution)/shard_map/all_to_all | solution.py:126
  44.1 0.6 %reduce_sum.9 = f32[8,128]{1,0:T(8,128)} reduce(f32[16,8,128]{2,1,0:T(8,128)S(1)} %all_to_all.11, f32[]{:T(128)} %constant.0.clone.1), dimensions={0}, to_apply=%region_0.0 | reduce | flops 15360 | bytes 69636 | tf_op jit(solution)/shard_map/reduce_sum | solution.py:127

commit v2 on v1

v2 whole, which is shorter than its diff:
```python
import functools
import math

import jax
import jax.numpy as jnp
from jax import lax
from jax.experimental import pallas as pl
from jax.experimental.pallas import tpu as pltpu
from jax.sharding import PartitionSpec as P

VMEM_LIMIT = 32 * 1024 * 1024


def pack_kernel(act_ref, grad_ref, tok_ref, out_ref):
    owners = out_ref.shape[0]
    rows = act_ref.shape[0]
    rank = act_ref.shape[1] // owners
    half = rows // 2
    examples, tokens = tok_ref.shape
    for owner in range(0, owners, 2):
        pair = slice(owner * rank, (owner + 2) * rank)
        turned = grad_ref[:, pair].T
        acts = act_ref[:, pair]
        for side in range(2):
            columns = slice(side * rank, (side + 1) * rank)
            out_ref[owner + side, :rank, :] = turned[columns, :]
            out_ref[owner + side, rank : rank + half, :] = jnp.concatenate(
                [acts[:half, columns], acts[half:, columns]], axis=1
            )
    tok = tok_ref[...]
    row_of_lane = lax.broadcasted_iota(jnp.int32, (examples, rows), 1)
    counts = jnp.zeros((examples, rows), jnp.float32)
    for t in range(tokens):
        counts += jnp.where(tok[:, t : t + 1] == row_of_lane, 1.0, 0.0)
    counts = counts.astype(jnp.bfloat16)
    for owner in range(owners):
        out_ref[owner, rank + half :, :] = counts


def query_kernel(query_ref, left_ref, right_ref, out_ref, diagonal, turned):
    rank = left_ref.shape[-1]
    tiles, _, lanes = turned.shape
    step = diagonal.shape[0]
    right = right_ref[0]
    diagonal[...] = jnp.zeros_like(diagonal)
    for at in range(0, step, rank):
        diagonal[at : at + rank, at : at + rank] = right
    left = left_ref[0].astype(jnp.float32).T.astype(jnp.bfloat16)
    left = jnp.concatenate([left, left], axis=1)
    for tile in range(tiles):
        columns = slice(tile * lanes, (tile + 1) * lanes)
        for at in range(0, rank * rank, step):
            turned[tile, at : at + step, :] = lax.dot_general(
                diagonal[...],
                query_ref[columns, at : at + step],
                (((1,), (1,)), ((), ())),
                preferred_element_type=jnp.float32,
            )
        for k in range(0, rank, 2):
            value = jnp.concatenate([turned[tile, pl.ds(k + s, rank, stride=rank), :] for s in range(2)], axis=1)
            high = value.astype(jnp.bfloat16)
            low = (value - high.astype(jnp.float32)).astype(jnp.bfloat16)
            product = jnp.dot(left, jnp.concatenate([high, low], axis=0), preferred_element_type=jnp.float32)
            for s in range(2):
                turned[tile, pl.ds(k + s, rank, stride=rank), :] = product[:, s * lanes : (s + 1) * lanes]
        out_ref[:, columns] = turned[tile].astype(jnp.bfloat16)


def owner_kernel(scale, recv, query, out_ref, grads, per_example):
    blocks, height, width = recv.shape
    rank = grads.shape[1]
    rows = width
    half_rows = rows // 2
    examples = height - rank - half_rows
    pairs = rank // 2
    first_half = lax.broadcasted_iota(jnp.int32, (half_rows, width), 1) < rank

    def one(b):
        counts = recv[b, rank + half_rows :, :].astype(jnp.float32)
        slot = b % grads.shape[0]
        grads[slot] = recv[b, :rank, :].astype(jnp.float32)
        acts = recv[b, rank : rank + half_rows, :]
        swapped = jnp.concatenate([acts[:, rank:], acts[:, :rank]], axis=1)
        zero = jnp.zeros_like(acts)
        weights = jnp.concatenate(
            [
                jnp.where(first_half, acts, zero),
                jnp.where(first_half, swapped, zero),
                jnp.where(first_half, zero, swapped),
                jnp.where(first_half, zero, acts),
            ],
            axis=0,
        )
        columns = []
        for parity in range(2):
            pieces = [grads[slot, pl.ds(2 * p + parity, 1), :] * counts for p in range(pairs)]
            columns.append(jnp.concatenate(pieces, axis=0).astype(jnp.bfloat16))
        weighted = jnp.concatenate(columns, axis=1)
        return jnp.dot(weighted, weights, preferred_element_type=jnp.float32) * scale

    for b in range(0, blocks, 2):
        first, second = one(b), one(b + 1)
        for p in range(pairs):
            piece = slice(p * examples, (p + 1) * examples)
            per_example[b * examples : (b + 2) * examples, p * width : (p + 1) * width] = jnp.concatenate(
                [first[piece], second[piece]], axis=0
            ).astype(jnp.bfloat16)

    out_ref[...] = jnp.dot(per_example[...], query[...], preferred_element_type=jnp.float32).T


def per_device(owners, act_table, grad_table, token_rows, left_inv, right_inv, query_grads):
    rows, columns = act_table.shape
    examples, tokens = token_rows.shape
    local_modules, rank, _ = left_inv.shape
    queries = query_grads.shape[0]
    width = 2 * rank
    lanes = min(queries, 128)
    assert queries % lanes == 0
    assert local_modules == 1 and columns == owners * rank and owners % 2 == 0
    assert rows == width and tokens <= 256 and examples % 8 == 0
    height = rank + rows // 2 + examples

    packed = pl.pallas_call(
        pack_kernel,
        out_shape=jax.ShapeDtypeStruct((owners, height, width), jnp.bfloat16),
        compiler_params=pltpu.CompilerParams(vmem_limit_bytes=VMEM_LIMIT),
        name="pack",
    )(act_table, grad_table, token_rows)
    recv = lax.all_to_all(packed, "module", split_axis=0, concat_axis=0, tiled=True)

    prepared = pl.pallas_call(
        query_kernel,
        out_shape=jax.ShapeDtypeStruct((rank * rank, queries), jnp.bfloat16),
        scratch_shapes=[
            pltpu.VMEM((4 * rank, 4 * rank), jnp.bfloat16),
            pltpu.VMEM((queries // lanes, rank * rank, lanes), jnp.float32),
        ],
        cost_estimate=pl.CostEstimate(
            flops=4 * queries * rank**3, bytes_accessed=4 * queries * rank**2, transcendentals=0
        ),
        compiler_params=pltpu.CompilerParams(vmem_limit_bytes=VMEM_LIMIT),
        name="prepare",
    )(query_grads.reshape(queries, rank * rank), left_inv, right_inv)

    partial = pl.pallas_call(
        functools.partial(owner_kernel, 1.0 / math.sqrt(tokens)),
        out_shape=jax.ShapeDtypeStruct((queries, owners * examples), jnp.float32),
        scratch_shapes=[
            pltpu.VMEM((4, rank, rows), jnp.float32),
            pltpu.VMEM((owners * examples, rank * rank), jnp.bfloat16),
        ],
        compiler_params=pltpu.CompilerParams(vmem_limit_bytes=VMEM_LIMIT),
        name="owner",
    )(recv, prepared)

    tiles = partial.reshape(owners, queries // owners, owners * examples)
    gathered = lax.all_to_all(tiles, "module", split_axis=0, concat_axis=0, tiled=True)
    return jnp.sum(gathered, axis=0)


def solution(mesh):
    placed = (
        P(("groups", "module"), None),
        P(("groups", "module"), None),
        P(("groups", "module"), None),
        P("module", None, None),
        P("module", None, None),
        P("groups", "module", None),
    )
    return jax.shard_map(
        functools.partial(per_device, mesh.shape["module"]),
        mesh=mesh,
        in_specs=placed,
        out_specs=P(("groups", "module"), None),
        check_vma=False,
    )
```

time: 45.2 us -> 39.5 us (0.87)
  blocking collectives: 34.6 us -> 11 us
  waiting for transfers between devices: 0 us -> 11.6 us
  starting transfers between devices: 0 us -> 7.55 us
  Pallas kernels: 9.57 us -> 5.61 us
  local copies, waits for them, and re-layouts: 0 us -> 2.69 us
    all_to_all x1 -> x0, blocking collectives: 24.2 us -> none  [per_device(): lax.all_to_all(packed, 'module', split_axis=0, concat_axis=0, tiled=True)]
    all_to_all x0 -> x1, waiting for transfers between devices: none -> 11.6 us  [per_device(): lax.all_to_all(packed, 'module', split_axis=0, concat_axis=0, tiled=True)]
    all_to_all x0 -> x1, starting transfers between devices: none -> 7.55 us  [per_device(): lax.all_to_all(packed, 'module', split_axis=0, concat_axis=0, tiled=True)]
    pallas_call x1, Pallas kernels: 7.31 us -> 1.16 us  [per_device(): pl.pallas_call(functools.partial(owner_kernel, 1.0 / math.sqrt(tokens)),...]
    pallas_call x0 -> x1, Pallas kernels: none -> 3.2 us  [per_device(): pl.pallas_call(query_kernel, out_shape=jax.ShapeDtypeStruct((rank * rank,...]
    unnamed x0 -> x12, local copies, waits for them, and re-layouts: none -> 2.69 us
    pallas_call x1, Pallas kernels: 2.26 us -> 1.24 us  [per_device(): pl.pallas_call(pack_kernel, out_shape=jax.ShapeDtypeStruct((owners, heigh...]
    all_to_all x1, blocking collectives: 10.4 us -> 11 us  [per_device(): lax.all_to_all(tiles, 'module', split_axis=0, concat_axis=0, tiled=True)]
  transfers between devices with their start and end apart: 0 -> 1, of which waited for: 0 -> 1; matrix products, arithmetic and copies ran while one was open for 0% -> 0% of each run, Pallas kernels for 0% -> 8%
where the time goes in v2:
time: 39.5 us; the launch traced here: 39.1 us
  waiting for transfers between devices  11.6 us (29%)
  blocking collectives  11 us (28%)
  starting transfers between devices  7.55 us (19%)
  Pallas kernels  5.61 us (14%)
  local copies, waits for them, and re-layouts  2.69 us (7%)
  other arithmetic  0.61 us (2%)
    all_to_all x1, waiting for transfers between devices, per_device(): lax.all_to_all(packed, 'module', split_axis=0, concat_axis=0, tiled=True)  11.6 us
    all_to_all x1, blocking collectives, per_device(): lax.all_to_all(tiles, 'module', split_axis=0, concat_axis=0, tiled=True)  11 us
    all_to_all x1, starting transfers between devices, per_device(): lax.all_to_all(packed, 'module', split_axis=0, concat_axis=0, tiled=True)  7.55 us
    pallas_call x1, Pallas kernels, per_device(): pl.pallas_call(query_kernel, out_shape=jax.ShapeDtypeStruct((rank * rank,...  3.2 us
    unnamed x12, local copies, waits for them, and re-layouts  2.69 us
    pallas_call x1, Pallas kernels, per_device(): pl.pallas_call(pack_kernel, out_shape=jax.ShapeDtypeStruct((owners, heigh...  1.24 us
    pallas_call x1, Pallas kernels, per_device(): pl.pallas_call(functools.partial(owner_kernel, 1.0 / math.sqrt(tokens)),...  1.16 us
  transfers between devices with their start and end apart: 1, of which 1 were waited for; matrix products, arithmetic and copies ran while one was open for 0% of the time, Pallas kernels for 8%

profile of v2, /device:TPU:0, one launch (start us, length us, event | category | flops | bytes accessed | tf_op | source)
XLA Modules:
  0.0 39.1 jit_solution(9629695103991583419)
XLA Ops:
  0.0 0.0 copy-start
  0.0 0.0 copy-start.1
  0.0 1.0 %copy-done.1 = bf16[128,1024]{1,0:T(8,128)(2,1)S(1)} copy-done((bf16[128,1024]{1,0:T(8,128)(2,1)S(1)}, bf16[128,1024]{1,0:T(8,128)(2,1)}, u32[]{:S(2)}) %copy-start.1) | copy-done | bytes 262168
  1.0 0.0 copy-start.2
  1.0 0.9 %copy-done.2 = bf16[128,1024]{1,0:T(8,128)(2,1)S(1)} copy-done((bf16[128,1024]{1,0:T(8,128)(2,1)S(1)}, bf16[128,1024]{1,0:T(8,128)(2,1)}, u32[]{:S(2)}) %copy-start.2) | copy-done | bytes 262168
  2.0 0.0 copy-start.5
  2.0 0.7 %copy-done.5 = s32[8,128]{1,0:T(8,128)S(1)} copy-done((s32[8,128]{1,0:T(8,128)S(1)}, s32[8,128]{1,0:T(8,128)}, u32[]{:S(2)}) %copy-start.5) | copy-done | bytes 4120
  2.7 1.2 %pack.1 = bf16[16,136,128]{2,1,0:T(8,128)(2,1)} custom-call(bf16[128,1024]{1,0:T(8,128)(2,1)S(1)} %copy-done.1, bf16[128,1024]{1,0:T(8,128)(2,1)S(1)} %copy-done.2, s32[8,128]{1,0:T(8,128)S(1)} %copy-done.5), custom_call_target="tpu_custom_call" | custom-call | tf_op jit(solution)/shard_map/pack/pallas_call | solution.py:124
  3.9 0.0 copy-start.3
  3.9 0.0 copy-start.4
  3.9 7.5 %all-to-all-start = ((bf16[16,136,128]{2,1,0:T(8,128)(2,1)}), bf16[16,136,128]{2,1,0:T(8,128)(2,1)S(1)}, u32[]{:S(2)}, u32[]{:S(2)}) async-start(bf16[16,136,128]{2,1,0:T(8,128)(2,1)} %pack.1), calls=%async_computation | async-start | bytes 1114112 | tf_op jit(solution)/shard_map/all_to_all | solution.py:130
  11.5 0.0 copy-done
  11.5 0.0 copy-done.3
  11.5 0.0 copy-done.4
  11.5 3.2 %prepare.1.query = bf16[4096,128]{1,0:T(8,128)(2,1)S(1)} custom-call(bf16[128,4096]{1,0:T(8,128)(2,1)S(1)} %bitcast.2, bf16[1,64,64]{2,1,0:T(8,128)(2,1)S(1)} %copy-done.3, bf16[1,64,64]{2,1,0:T(8,128)(2,1)S(1)} %copy-done.4), custom_call_target="tpu_custom_call" | custom-call | flops 134217728 | bytes 2097152 | tf_op jit(solution)/shard_map/prepare/pallas_call | solution.py:132
  14.7 11.6 %all-to-all-done.recv = bf16[16,136,128]{2,1,0:T(8,128)(2,1)S(1)} async-done(((bf16[16,136,128]{2,1,0:T(8,128)(2,1)}), bf16[16,136,128]{2,1,0:T(8,128)(2,1)S(1)}, u32[]{:S(2)}, u32[]{:S(2)}) %all-to-all-start) | async-done | bytes 557088 | tf_op jit(solution)/shard_map/all_to_all | solution.py:130
  26.3 1.2 %owner.1 = f32[128,128]{1,0:T(8,128)S(1)} custom-call(bf16[16,136,128]{2,1,0:T(8,128)(2,1)S(1)} %all-to-all-done.recv, bf16[4096,128]{1,0:T(8,128)(2,1)S(1)} %prepare.1.query), custom_call_target="tpu_custom_call" | custom-call | tf_op jit(solution)/shard_map/owner/pallas_call | solution.py:146
  27.5 11.0 %all_to_all.10 = f32[16,8,128]{2,1,0:T(8,128)S(1)} all-to-all(f32[16,8,128]{2,1,0:T(8,128)S(1)} %bitcast.3), channel_id=1, replica_groups=mesh['groups'=2,'module'=16] {'module'}, dimensions={0} | all-to-all | bytes 131072 | tf_op jit(solution)/shard_map/all_to_all | solution.py:158
  38.5 0.6 %reduce_sum.9 = f32[8,128]{1,0:T(8,128)} reduce(f32[16,8,128]{2,1,0:T(8,128)S(1)} %all_to_all.10, f32[]{:T(128)} %constant.0.clone.1), dimensions={0}, to_apply=%region_0.0 | reduce | flops 15360 | bytes 69636 | tf_op jit(solution)/shard_map/reduce_sum | solution.py:159
Async XLA Ops:
  0.0 11.5 %copy-start = (bf16[128,1,4096]{2,0,1:T(8,128)(2,1)S(1)}, bf16[128,1,4096]{2,0,1:T(8,128)(2,1)}, u32[]{:S(2)}) copy-start(bf16[128,1,4096]{2,0,1:T(8,128)(2,1)} %param.11) | copy-start | bytes 3145732
  0.0 1.0 %copy-start.1 = (bf16[128,1024]{1,0:T(8,128)(2,1)S(1)}, bf16[128,1024]{1,0:T(8,128)(2,1)}, u32[]{:S(2)}) copy-start(bf16[128,1024]{1,0:T(8,128)(2,1)} %act_ref.1) | copy-start | bytes 786436
  1.0 0.9 %copy-start.2 = (bf16[128,1024]{1,0:T(8,128)(2,1)S(1)}, bf16[128,1024]{1,0:T(8,128)(2,1)}, u32[]{:S(2)}) copy-start(bf16[128,1024]{1,0:T(8,128)(2,1)} %grad_ref.1) | copy-start | bytes 786436
  2.0 0.7 %copy-start.5 = (s32[8,128]{1,0:T(8,128)S(1)}, s32[8,128]{1,0:T(8,128)}, u32[]{:S(2)}) copy-start(s32[8,128]{1,0:T(8,128)} %tok_ref.1) | copy-start | bytes 12292
  3.9 7.6 %copy-start.3 = (bf16[1,64,64]{2,1,0:T(8,128)(2,1)S(1)}, bf16[1,64,64]{2,1,0:T(8,128)(2,1)}, u32[]{:S(2)}) copy-start(bf16[1,64,64]{2,1,0:T(8,128)(2,1)} %left_ref.1) | copy-start | bytes 24580
  3.9 7.6 %copy-start.4 = (bf16[1,64,64]{2,1,0:T(8,128)(2,1)S(1)}, bf16[1,64,64]{2,1,0:T(8,128)(2,1)}, u32[]{:S(2)}) copy-start(bf16[1,64,64]{2,1,0:T(8,128)(2,1)} %right_ref.1) | copy-start | bytes 24580
  3.9 22.4 %all-to-all-start = ((bf16[16,136,128]{2,1,0:T(8,128)(2,1)}), bf16[16,136,128]{2,1,0:T(8,128)(2,1)S(1)}, u32[]{:S(2)}, u32[]{:S(2)}) async-start(bf16[16,136,128]{2,1,0:T(8,128)(2,1)} %pack.1), calls=%async_computation | async-start | bytes 1114112 | tf_op jit(solution)/shard_map/all_to_all | solution.py:130

commit v3 on v2

--- a/solution.py
+++ b/solution.py
@@ -9,32 +9,68 @@
 from jax.sharding import PartitionSpec as P
 
 VMEM_LIMIT = 32 * 1024 * 1024
-
-
-def pack_kernel(act_ref, grad_ref, tok_ref, out_ref):
-    owners = out_ref.shape[0]
-    rows = act_ref.shape[0]
-    rank = act_ref.shape[1] // owners
+CHUNKS = 2
+
+
+def member_order(members):
+    first = members * 11 // 16
+
+    def hops(i):
+        return abs((i >> 2) - (first >> 2)) + (((i ^ first) >> 1) & 1)
+
+    return [first] + sorted((i for i in range(members) if i != first), key=lambda i: (-hops(i), i))
+
+
+def pack_kernel(slots, act_hbm, grad_hbm, tok_hbm, out_hbm, act, grad, tok, packed, in_sem, out_sem):
+    owners = out_hbm.shape[0]
+    rows = act.shape[0]
+    rank = act.shape[1] // owners
     half = rows // 2
-    examples, tokens = tok_ref.shape
-    for owner in range(0, owners, 2):
-        pair = slice(owner * rank, (owner + 2) * rank)
-        turned = grad_ref[:, pair].T
-        acts = act_ref[:, pair]
-        for side in range(2):
-            columns = slice(side * rank, (side + 1) * rank)
-            out_ref[owner + side, :rank, :] = turned[columns, :]
-            out_ref[owner + side, rank : rank + half, :] = jnp.concatenate(
-                [acts[:half, columns], acts[half:, columns]], axis=1
-            )
-    tok = tok_ref[...]
+    examples, tokens = tok.shape
+    chunks = in_sem.shape[0] // 2
+    share = owners // chunks
+    arrivals = []
+    tok_copy = pltpu.make_async_copy(tok_hbm, tok, in_sem.at[2 * chunks])
+    tok_copy.start()
+    for c in range(chunks):
+        columns = pl.ds(c * share * rank, share * rank)
+        pair = [
+            pltpu.make_async_copy(grad_hbm.at[:, columns], grad.at[:, columns], in_sem.at[2 * c]),
+            pltpu.make_async_copy(act_hbm.at[:, columns], act.at[:, columns], in_sem.at[2 * c + 1]),
+        ]
+        for copy in pair:
+            copy.start()
+        arrivals.append(pair)
+
+    tok_copy.wait()
+    local = tok[...]
     row_of_lane = lax.broadcasted_iota(jnp.int32, (examples, rows), 1)
     counts = jnp.zeros((examples, rows), jnp.float32)
     for t in range(tokens):
-        counts += jnp.where(tok[:, t : t + 1] == row_of_lane, 1.0, 0.0)
+        counts += jnp.where(local[:, t : t + 1] == row_of_lane, 1.0, 0.0)
     counts = counts.astype(jnp.bfloat16)
-    for owner in range(owners):
-        out_ref[owner, rank + half :, :] = counts
+
+    departures = []
+    for c in range(chunks):
+        for copy in arrivals[c]:
+            copy.wait()
+        for owner in range(c * share, (c + 1) * share, 2):
+            pair = slice(owner * rank, (owner + 2) * rank)
+            turned = grad[:, pair].T
+            acts = act[:, pair]
+            for side in range(2):
+                columns = slice(side * rank, (side + 1) * rank)
+                packed[owner + side, :rank, :] = turned[columns, :]
+                packed[owner + side, rank : rank + half, :] = jnp.concatenate(
+                    [acts[:half, columns], acts[half:, columns]], axis=1
+                )
+                packed[owner + side, rank + half :, :] = counts
+        for owner in range(c * share, (c + 1) * share):
+            copy = pltpu.make_async_copy(packed.at[owner], out_hbm.at[slots[owner]], out_sem.at[owner])
+            copy.start()
+            departures.append(copy)
+    for copy in departures:
+        copy.wait()
 
 
 def query_kernel(query_ref, left_ref, right_ref, out_ref, diagonal, turned):
@@ -66,7 +102,7 @@
         out_ref[:, columns] = turned[tile].astype(jnp.bfloat16)
 
 
-def owner_kernel(scale, recv, query, out_ref, grads, per_example):
+def owner_kernel(scale, order, slots, recv, query, out_ref, grads, per_example):
     blocks, height, width = recv.shape
     rank = grads.shape[1]
     rows = width
@@ -99,14 +135,17 @@
         return jnp.dot(weighted, weights, preferred_element_type=jnp.float32) * scale
 
     for b in range(0, blocks, 2):
-        first, second = one(b), one(b + 1)
+        first, second = one(slots[b]), one(slots[b + 1])
         for p in range(pairs):
             piece = slice(p * examples, (p + 1) * examples)
             per_example[b * examples : (b + 2) * examples, p * width : (p + 1) * width] = jnp.concatenate(
                 [first[piece], second[piece]], axis=0
             ).astype(jnp.bfloat16)
 
-    out_ref[...] = jnp.dot(per_example[...], query[...], preferred_element_type=jnp.float32).T
+    scores = jnp.dot(per_example[...], query[...], preferred_element_type=jnp.float32).T
+    tile = out_ref.shape[1]
+    for slot, member in enumerate(order):
+        out_ref[slot] = scores[member * tile : (member + 1) * tile]
 
 
 def per_device(owners, act_table, grad_table, token_rows, left_inv, right_inv, query_grads):
@@ -120,14 +159,32 @@
     assert local_modules == 1 and columns == owners * rank and owners % 2 == 0
     assert rows == width and tokens <= 256 and examples % 8 == 0
     height = rank + rows // 2 + examples
+    chunks = math.gcd(CHUNKS, owners // 2)
+
+    order = member_order(owners)
+    slots = [order.index(member) for member in range(owners)]
+
+    def exchange(pieces):
+        return lax.all_to_all(
+            pieces, "module", split_axis=0, concat_axis=0, axis_index_groups=[order], tiled=True
+        )
 
     packed = pl.pallas_call(
-        pack_kernel,
+        functools.partial(pack_kernel, slots),
         out_shape=jax.ShapeDtypeStruct((owners, height, width), jnp.bfloat16),
-        compiler_params=pltpu.CompilerParams(vmem_limit_bytes=VMEM_LIMIT),
+        in_specs=[pl.BlockSpec(memory_space=pltpu.HBM)] * 3,
+        out_specs=pl.BlockSpec(memory_space=pltpu.HBM),
+        scratch_shapes=[
+            pltpu.VMEM((rows, columns), jnp.bfloat16),
+            pltpu.VMEM((rows, columns), jnp.bfloat16),
+            pltpu.VMEM((examples, tokens), jnp.int32),
+            pltpu.VMEM((owners, height, width), jnp.bfloat16),
+            pltpu.SemaphoreType.DMA((2 * chunks + 1,)),
+            pltpu.SemaphoreType.DMA((owners,)),
+        ],
         name="pack",
     )(act_table, grad_table, token_rows)
-    recv = lax.all_to_all(packed, "module", split_axis=0, concat_axis=0, tiled=True)
+    recv = exchange(packed)
 
     prepared = pl.pallas_call(
         query_kernel,
@@ -144,8 +201,8 @@
     )(query_grads.reshape(queries, rank * rank), left_inv, right_inv)
 
     partial = pl.pallas_call(
-        functools.partial(owner_kernel, 1.0 / math.sqrt(tokens)),
-        out_shape=jax.ShapeDtypeStruct((queries, owners * examples), jnp.float32),
+        functools.partial(owner_kernel, 1.0 / math.sqrt(tokens), order, slots),
+        out_shape=jax.ShapeDtypeStruct((owners, queries // owners, owners * examples), jnp.float32),
         scratch_shapes=[
             pltpu.VMEM((4, rank, rows), jnp.float32),
             pltpu.VMEM((owners * examples, rank * rank), jnp.bfloat16),
@@ -154,9 +211,7 @@
         name="owner",
     )(recv, prepared)
 
-    tiles = partial.reshape(owners, queries // owners, owners * examples)
-    gathered = lax.all_to_all(tiles, "module", split_axis=0, concat_axis=0, tiled=True)
-    return jnp.sum(gathered, axis=0)
+    return jnp.sum(exchange(partial), axis=0)
 
 
 def solution(mesh):

time: 39.5 us -> 33.9 us (0.86)
  blocking collectives: 11 us -> 8.17 us
  local copies, waits for them, and re-layouts: 2.69 us -> 0.02 us
  waiting for transfers between devices: 11.6 us -> 10.3 us
  Pallas kernels: 5.61 us -> 6.62 us
    all_to_all x1, blocking collectives: 11 us -> 8.17 us  [exchange(): lax.all_to_all(pieces, 'module', split_axis=0, concat_axis=0, axis_index_...]
    unnamed x12 -> x6, local copies, waits for them, and re-layouts: 2.69 us -> 0.02 us
    all_to_all x1, waiting for transfers between devices: 11.6 us -> 10.3 us  [exchange(): lax.all_to_all(pieces, 'module', split_axis=0, concat_axis=0, axis_index_...]
    pallas_call x2, Pallas kernels: 2.4 us -> 3.42 us  [the longest x1 2.25 us: per_device(): pl.pallas_call(functools.partial(pack_kernel, slots), out_shape=jax.Shape...]
  transfers between devices with their start and end apart: 1 -> 1, of which waited for: 1 -> 1; matrix products, arithmetic and copies ran while one was open for 0% -> 0% of each run, Pallas kernels for 8% -> 10%
where the time goes in v3:
time: 33.9 us; the launch traced here: 33.6 us
  waiting for transfers between devices  10.3 us (30%)
  blocking collectives  8.17 us (24%)
  starting transfers between devices  7.84 us (23%)
  Pallas kernels  6.62 us (20%)
  other arithmetic  0.61 us (2%)
    all_to_all x1, waiting for transfers between devices, exchange(): lax.all_to_all(pieces, 'module', split_axis=0, concat_axis=0, axis_index_...  10.3 us
    all_to_all x1, blocking collectives, exchange(): lax.all_to_all(pieces, 'module', split_axis=0, concat_axis=0, axis_index_...  8.17 us
    all_to_all x1, starting transfers between devices, exchange(): lax.all_to_all(pieces, 'module', split_axis=0, concat_axis=0, axis_index_...  7.84 us
    pallas_call x1, Pallas kernels, per_device(): pl.pallas_call(query_kernel, out_shape=jax.ShapeDtypeStruct((rank * rank,...  3.2 us
    pallas_call x1, Pallas kernels, per_device(): pl.pallas_call(functools.partial(pack_kernel, slots), out_shape=jax.Shape...  2.25 us
    pallas_call x1, Pallas kernels, per_device(): pl.pallas_call(functools.partial(owner_kernel, 1.0 / math.sqrt(tokens), o...  1.17 us
  transfers between devices with their start and end apart: 1, of which 1 were waited for; matrix products, arithmetic and copies ran while one was open for 0% of the time, Pallas kernels for 10%

profile of v3, /device:TPU:0, one launch (start us, length us, event | category | flops | bytes accessed | tf_op | source)
XLA Modules:
  0.0 33.6 jit_solution(1613511071869508139)
XLA Ops:
  0.0 0.0 copy-start
  0.0 2.3 %pack.1 = bf16[16,136,128]{2,1,0:T(8,128)(2,1)} custom-call(bf16[128,1024]{1,0:T(8,128)(2,1)} %act_hbm.1, bf16[128,1024]{1,0:T(8,128)(2,1)} %grad_hbm.1, s32[8,128]{1,0:T(8,128)} %tok_hbm.1), custom_call_target="tpu_custom_call" | custom-call | tf_op jit(solution)/shard_map/pack/pallas_call | solution.py:172
  2.3 0.0 copy-start.1
  2.3 0.0 copy-start.2
  2.3 7.8 %all-to-all-start = ((bf16[16,136,128]{2,1,0:T(8,128)(2,1)}), bf16[16,136,128]{2,1,0:T(8,128)(2,1)S(1)}, u32[]{:S(2)}, u32[]{:S(2)}) async-start(bf16[16,136,128]{2,1,0:T(8,128)(2,1)} %pack.1), calls=%async_computation | async-start | bytes 1114112 | tf_op jit(solution)/shard_map/all_to_all | solution.py:168
  10.1 0.0 copy-done
  10.1 0.0 copy-done.1
  10.1 0.0 copy-done.2
  10.2 3.2 %prepare.1.query = bf16[4096,128]{1,0:T(8,128)(2,1)S(1)} custom-call(bf16[128,4096]{1,0:T(8,128)(2,1)S(1)} %bitcast.1, bf16[1,64,64]{2,1,0:T(8,128)(2,1)S(1)} %copy-done.1, bf16[1,64,64]{2,1,0:T(8,128)(2,1)S(1)} %copy-done.2), custom_call_target="tpu_custom_call" | custom-call | flops 134217728 | bytes 2097152 | tf_op jit(solution)/shard_map/prepare/pallas_call | solution.py:189
  13.4 10.3 %all-to-all-done.recv = bf16[16,136,128]{2,1,0:T(8,128)(2,1)S(1)} async-done(((bf16[16,136,128]{2,1,0:T(8,128)(2,1)}), bf16[16,136,128]{2,1,0:T(8,128)(2,1)S(1)}, u32[]{:S(2)}, u32[]{:S(2)}) %all-to-all-start) | async-done | bytes 557088 | tf_op jit(solution)/shard_map/all_to_all | solution.py:168
  23.6 1.2 %owner.1 = f32[16,8,128]{2,1,0:T(8,128)S(1)} custom-call(bf16[16,136,128]{2,1,0:T(8,128)(2,1)S(1)} %all-to-all-done.recv, bf16[4096,128]{1,0:T(8,128)(2,1)S(1)} %prepare.1.query), custom_call_target="tpu_custom_call" | custom-call | tf_op jit(solution)/shard_map/owner/pallas_call | solution.py:203
  24.8 8.2 %all_to_all.10 = f32[16,8,128]{2,1,0:T(8,128)S(1)} all-to-all(f32[16,8,128]{2,1,0:T(8,128)S(1)} %owner.1), channel_id=1, replica_groups={{11,0,1,2,3,4,5,12,13,6,7,8,9,14,15,10},{27,16,17,18,19,20,21,28,29,22,..., dimensions={0} | all-to-all | bytes 131072 | tf_op jit(solution)/shard_map/all_to_all | solution.py:168
  33.0 0.6 %reduce_sum.9 = f32[8,128]{1,0:T(8,128)} reduce(f32[16,8,128]{2,1,0:T(8,128)S(1)} %all_to_all.10, f32[]{:T(128)} %constant.0.clone.1), dimensions={0}, to_apply=%region_0.0 | reduce | flops 15360 | bytes 69636 | tf_op jit(solution)/shard_map/reduce_sum | solution.py:214
Async XLA Ops:
  0.0 10.1 %copy-start = (bf16[128,1,4096]{2,0,1:T(8,128)(2,1)S(1)}, bf16[128,1,4096]{2,0,1:T(8,128)(2,1)}, u32[]{:S(2)}) copy-start(bf16[128,1,4096]{2,0,1:T(8,128)(2,1)} %param.11) | copy-start | bytes 3145732
  2.3 7.9 %copy-start.1 = (bf16[1,64,64]{2,1,0:T(8,128)(2,1)S(1)}, bf16[1,64,64]{2,1,0:T(8,128)(2,1)}, u32[]{:S(2)}) copy-start(bf16[1,64,64]{2,1,0:T(8,128)(2,1)} %left_ref.1) | copy-start | bytes 24580
  2.3 7.9 %copy-start.2 = (bf16[1,64,64]{2,1,0:T(8,128)(2,1)S(1)}, bf16[1,64,64]{2,1,0:T(8,128)(2,1)}, u32[]{:S(2)}) copy-start(bf16[1,64,64]{2,1,0:T(8,128)(2,1)} %right_ref.1) | copy-start | bytes 24580
  2.3 21.3 %all-to-all-start = ((bf16[16,136,128]{2,1,0:T(8,128)(2,1)}), bf16[16,136,128]{2,1,0:T(8,128)(2,1)S(1)}, u32[]{:S(2)}, u32[]{:S(2)}) async-start(bf16[16,136,128]{2,1,0:T(8,128)(2,1)} %pack.1), calls=%async_computation | async-start | bytes 1114112 | tf_op jit(solution)/shard_map/all_to_all | solution.py:168

commit v4 on v3

--- a/solution.py
+++ b/solution.py
@@ -9,12 +9,10 @@
 from jax.sharding import PartitionSpec as P
 
 VMEM_LIMIT = 32 * 1024 * 1024
-CHUNKS = 2
-
-
-def member_order(members):
-    first = members * 11 // 16
-
+FIRST_OUT, FIRST_BACK = 9, 11
+
+
+def member_order(members, first):
     def hops(i):
         return abs((i >> 2) - (first >> 2)) + (((i ^ first) >> 1) & 1)
 
@@ -27,20 +25,12 @@
     rank = act.shape[1] // owners
     half = rows // 2
     examples, tokens = tok.shape
-    chunks = in_sem.shape[0] // 2
-    share = owners // chunks
-    arrivals = []
-    tok_copy = pltpu.make_async_copy(tok_hbm, tok, in_sem.at[2 * chunks])
+    tok_copy = pltpu.make_async_copy(tok_hbm, tok, in_sem.at[0])
+    grad_copy = pltpu.make_async_copy(grad_hbm, grad, in_sem.at[1])
+    act_copy = pltpu.make_async_copy(act_hbm, act, in_sem.at[2])
     tok_copy.start()
-    for c in range(chunks):
-        columns = pl.ds(c * share * rank, share * rank)
-        pair = [
-            pltpu.make_async_copy(grad_hbm.at[:, columns], grad.at[:, columns], in_sem.at[2 * c]),
-            pltpu.make_async_copy(act_hbm.at[:, columns], act.at[:, columns], in_sem.at[2 * c + 1]),
-        ]
-        for copy in pair:
-            copy.start()
-        arrivals.append(pair)
+    grad_copy.start()
+    act_copy.start()
 
     tok_copy.wait()
     local = tok[...]
@@ -50,25 +40,28 @@
         counts += jnp.where(local[:, t : t + 1] == row_of_lane, 1.0, 0.0)
     counts = counts.astype(jnp.bfloat16)
 
+    grad_copy.wait()
+    act_copy.wait()
     departures = []
-    for c in range(chunks):
-        for copy in arrivals[c]:
-            copy.wait()
-        for owner in range(c * share, (c + 1) * share, 2):
-            pair = slice(owner * rank, (owner + 2) * rank)
-            turned = grad[:, pair].T
-            acts = act[:, pair]
+    ready = set()
+    share = owners // out_sem.shape[0]
+    for slot in range(owners):
+        pair = slots.index(slot) // 2
+        if pair not in ready:
+            ready.add(pair)
+            wide = slice(2 * pair * rank, 2 * (pair + 1) * rank)
+            turned = grad[:, wide].T
+            acts = act[:, wide]
             for side in range(2):
                 columns = slice(side * rank, (side + 1) * rank)
-                packed[owner + side, :rank, :] = turned[columns, :]
-                packed[owner + side, rank : rank + half, :] = jnp.concatenate(
-                    [acts[:half, columns], acts[half:, columns]], axis=1
-                )
-                packed[owner + side, rank + half :, :] = counts
-        for owner in range(c * share, (c + 1) * share):
-            copy = pltpu.make_async_copy(packed.at[owner], out_hbm.at[slots[owner]], out_sem.at[owner])
-            copy.start()
-            departures.append(copy)
+                to = slots[2 * pair + side]
+                packed[to, :rank, :] = turned[columns, :]
+                packed[to, rank : rank + half, :] = jnp.concatenate([acts[:half, columns], acts[half:, columns]], axis=1)
+                packed[to, rank + half :, :] = counts
+        if (slot + 1) % share == 0:
+            block = pl.ds(slot + 1 - share, share)
+            departures.append(pltpu.make_async_copy(packed.at[block], out_hbm.at[block], out_sem.at[slot // share]))
+            departures[-1].start()
     for copy in departures:
         copy.wait()
 
@@ -159,12 +152,12 @@
     assert local_modules == 1 and columns == owners * rank and owners % 2 == 0
     assert rows == width and tokens <= 256 and examples % 8 == 0
     height = rank + rows // 2 + examples
-    chunks = math.gcd(CHUNKS, owners // 2)
-
-    order = member_order(owners)
+
+    order = member_order(owners, owners * FIRST_OUT // 16)
+    back = member_order(owners, owners * FIRST_BACK // 16)
     slots = [order.index(member) for member in range(owners)]
 
-    def exchange(pieces):
+    def exchange(pieces, order):
         return lax.all_to_all(
             pieces, "module", split_axis=0, concat_axis=0, axis_index_groups=[order], tiled=True
         )
@@ -179,12 +172,12 @@
             pltpu.VMEM((rows, columns), jnp.bfloat16),
             pltpu.VMEM((examples, tokens), jnp.int32),
             pltpu.VMEM((owners, height, width), jnp.bfloat16),
-            pltpu.SemaphoreType.DMA((2 * chunks + 1,)),
-            pltpu.SemaphoreType.DMA((owners,)),
+            pltpu.SemaphoreType.DMA((3,)),
+            pltpu.SemaphoreType.DMA((2,)),
         ],
         name="pack",
     )(act_table, grad_table, token_rows)
-    recv = exchange(packed)
+    recv = exchange(packed, order)
 
     prepared = pl.pallas_call(
         query_kernel,
@@ -201,7 +194,7 @@
     )(query_grads.reshape(queries, rank * rank), left_inv, right_inv)
 
     partial = pl.pallas_call(
-        functools.partial(owner_kernel, 1.0 / math.sqrt(tokens), order, slots),
+        functools.partial(owner_kernel, 1.0 / math.sqrt(tokens), back, slots),
         out_shape=jax.ShapeDtypeStruct((owners, queries // owners, owners * examples), jnp.float32),
         scratch_shapes=[
             pltpu.VMEM((4, rank, rows), jnp.float32),
@@ -211,7 +204,7 @@
         name="owner",
     )(recv, prepared)
 
-    return jnp.sum(exchange(partial), axis=0)
+    return jnp.sum(exchange(partial, back), axis=0)
 
 
 def solution(mesh):

time: 33.9 us -> 33.5 us (0.988)
  waiting for transfers between devices: 10.3 us -> 7.22 us
  blocking collectives: 8.17 us -> 11.2 us
    all_to_all x1, waiting for transfers between devices: 10.3 us -> 7.22 us  [exchange(): lax.all_to_all(pieces, 'module', split_axis=0, concat_axis=0, axis_index_...]
    all_to_all x1, blocking collectives: 8.17 us -> 11.2 us  [exchange(): lax.all_to_all(pieces, 'module', split_axis=0, concat_axis=0, axis_index_...]
where the time goes in v4:
time: 33.5 us; the launch traced here: 33.2 us
  blocking collectives  11.2 us (33%)
  starting transfers between devices  7.62 us (23%)
  waiting for transfers between devices  7.22 us (22%)
  Pallas kernels  6.51 us (19%)
  other arithmetic  0.61 us (2%)
    all_to_all x1, blocking collectives, exchange(): lax.all_to_all(pieces, 'module', split_axis=0, concat_axis=0, axis_index_...  11.2 us
    all_to_all x1, starting transfers between devices, exchange(): lax.all_to_all(pieces, 'module', split_axis=0, concat_axis=0, axis_index_...  7.62 us
    all_to_all x1, waiting for transfers between devices, exchange(): lax.all_to_all(pieces, 'module', split_axis=0, concat_axis=0, axis_index_...  7.22 us
    pallas_call x1, Pallas kernels, per_device(): pl.pallas_call(query_kernel, out_shape=jax.ShapeDtypeStruct((rank * rank,...  3.2 us
    pallas_call x1, Pallas kernels, per_device(): pl.pallas_call(functools.partial(pack_kernel, slots), out_shape=jax.Shape...  2.14 us
    pallas_call x1, Pallas kernels, per_device(): pl.pallas_call(functools.partial(owner_kernel, 1.0 / math.sqrt(tokens), b...  1.17 us
  transfers between devices with their start and end apart: 1, of which 1 were waited for; matrix products, arithmetic and copies ran while one was open for 0% of the time, Pallas kernels for 10%

profile of v4, /device:TPU:0, one launch (start us, length us, event | category | flops | bytes accessed | tf_op | source)
XLA Modules:
  0.0 33.2 jit_solution(10203985627258639968)
XLA Ops:
  0.0 0.0 copy-start
  0.0 2.1 %pack.1 = bf16[16,136,128]{2,1,0:T(8,128)(2,1)} custom-call(bf16[128,1024]{1,0:T(8,128)(2,1)} %act_hbm.1, bf16[128,1024]{1,0:T(8,128)(2,1)} %grad_hbm.1, s32[8,128]{1,0:T(8,128)} %tok_hbm.1), custom_call_target="tpu_custom_call" | custom-call | tf_op jit(solution)/shard_map/pack/pallas_call | solution.py:165
  2.1 0.0 copy-start.1
  2.2 0.0 copy-start.2
  2.2 7.6 %all-to-all-start = ((bf16[16,136,128]{2,1,0:T(8,128)(2,1)}), bf16[16,136,128]{2,1,0:T(8,128)(2,1)S(1)}, u32[]{:S(2)}, u32[]{:S(2)}) async-start(bf16[16,136,128]{2,1,0:T(8,128)(2,1)} %pack.1), calls=%async_computation | async-start | bytes 1114112 | tf_op jit(solution)/shard_map/all_to_all | solution.py:161
  9.8 0.0 copy-done
  9.8 0.0 copy-done.1
  9.8 0.0 copy-done.2
  9.8 3.2 %prepare.1.query = bf16[4096,128]{1,0:T(8,128)(2,1)S(1)} custom-call(bf16[128,4096]{1,0:T(8,128)(2,1)S(1)} %bitcast.1, bf16[1,64,64]{2,1,0:T(8,128)(2,1)S(1)} %copy-done.1, bf16[1,64,64]{2,1,0:T(8,128)(2,1)S(1)} %copy-done.2), custom_call_target="tpu_custom_call" | custom-call | flops 134217728 | bytes 2097152 | tf_op jit(solution)/shard_map/prepare/pallas_call | solution.py:182
  13.0 7.2 %all-to-all-done.recv = bf16[16,136,128]{2,1,0:T(8,128)(2,1)S(1)} async-done(((bf16[16,136,128]{2,1,0:T(8,128)(2,1)}), bf16[16,136,128]{2,1,0:T(8,128)(2,1)S(1)}, u32[]{:S(2)}, u32[]{:S(2)}) %all-to-all-start) | async-done | bytes 557088 | tf_op jit(solution)/shard_map/all_to_all | solution.py:161
  20.3 1.2 %owner.1 = f32[16,8,128]{2,1,0:T(8,128)S(1)} custom-call(bf16[16,136,128]{2,1,0:T(8,128)(2,1)S(1)} %all-to-all-done.recv, bf16[4096,128]{1,0:T(8,128)(2,1)S(1)} %prepare.1.query), custom_call_target="tpu_custom_call" | custom-call | tf_op jit(solution)/shard_map/owner/pallas_call | solution.py:196
  21.4 11.2 %all_to_all.10 = f32[16,8,128]{2,1,0:T(8,128)S(1)} all-to-all(f32[16,8,128]{2,1,0:T(8,128)S(1)} %owner.1), channel_id=1, replica_groups={{11,0,1,2,3,4,5,12,13,6,7,8,9,14,15,10},{27,16,17,18,19,20,21,28,29,22,..., dimensions={0} | all-to-all | bytes 131072 | tf_op jit(solution)/shard_map/all_to_all | solution.py:161
  32.6 0.6 %reduce_sum.9 = f32[8,128]{1,0:T(8,128)} reduce(f32[16,8,128]{2,1,0:T(8,128)S(1)} %all_to_all.10, f32[]{:T(128)} %constant.0.clone.1), dimensions={0}, to_apply=%region_0.0 | reduce | flops 15360 | bytes 69636 | tf_op jit(solution)/shard_map/reduce_sum | solution.py:207
Async XLA Ops:
  0.0 9.8 %copy-start = (bf16[128,1,4096]{2,0,1:T(8,128)(2,1)S(1)}, bf16[128,1,4096]{2,0,1:T(8,128)(2,1)}, u32[]{:S(2)}) copy-start(bf16[128,1,4096]{2,0,1:T(8,128)(2,1)} %param.11) | copy-start | bytes 3145732
  2.1 7.7 %copy-start.1 = (bf16[1,64,64]{2,1,0:T(8,128)(2,1)S(1)}, bf16[1,64,64]{2,1,0:T(8,128)(2,1)}, u32[]{:S(2)}) copy-start(bf16[1,64,64]{2,1,0:T(8,128)(2,1)} %left_ref.1) | copy-start | bytes 24580
  2.2 7.6 %copy-start.2 = (bf16[1,64,64]{2,1,0:T(8,128)(2,1)S(1)}, bf16[1,64,64]{2,1,0:T(8,128)(2,1)}, u32[]{:S(2)}) copy-start(bf16[1,64,64]{2,1,0:T(8,128)(2,1)} %right_ref.1) | copy-start | bytes 24580
  2.2 18.1 %all-to-all-start = ((bf16[16,136,128]{2,1,0:T(8,128)(2,1)}), bf16[16,136,128]{2,1,0:T(8,128)(2,1)S(1)}, u32[]{:S(2)}, u32[]{:S(2)}) async-start(bf16[16,136,128]{2,1,0:T(8,128)(2,1)} %pack.1), calls=%async_computation | async-start | bytes 1114112 | tf_op jit(solution)/shard_map/all_to_all | solution.py:161

commit v5 on v4

v5 whole, which is shorter than its diff:
```python
import functools
import math

import jax
import jax.numpy as jnp
from jax import lax
from jax.experimental import pallas as pl
from jax.experimental.pallas import tpu as pltpu
from jax.sharding import PartitionSpec as P


VMEM_LIMIT = 32 * 1024 * 1024
FIRST_OUT, FIRST_BACK = 9, 11
MOST_HOPPING = 16


def member_order(members, first):
    def hops(i):
        return abs((i >> 2) - (first >> 2)) + (((i ^ first) >> 1) & 1)

    return [first] + sorted((i for i in range(members) if i != first), key=lambda i: (-hops(i), i))


def pack_kernel(slots, act_hbm, grad_hbm, tok_hbm, out_hbm, act, grad, tok, packed, in_sem, out_sem):
    owners = out_hbm.shape[0]
    rows = act.shape[0]
    rank = act.shape[1] // owners
    half = rows // 2
    examples, tokens = tok.shape
    tok_copy = pltpu.make_async_copy(tok_hbm, tok, in_sem.at[0])
    grad_copy = pltpu.make_async_copy(grad_hbm, grad, in_sem.at[1])
    act_copy = pltpu.make_async_copy(act_hbm, act, in_sem.at[2])
    tok_copy.start()
    grad_copy.start()
    act_copy.start()

    tok_copy.wait()
    local = tok[...]
    row_of_lane = lax.broadcasted_iota(jnp.int32, (examples, rows), 1)
    counts = jnp.zeros((examples, rows), jnp.float32)
    for t in range(tokens):
        counts += jnp.where(local[:, t : t + 1] == row_of_lane, 1.0, 0.0)
    counts = counts.astype(jnp.bfloat16)

    grad_copy.wait()
    act_copy.wait()
    departures = []
    ready = set()
    share = owners // out_sem.shape[0]
    for slot in range(owners):
        pair = slots.index(slot) // 2
        if pair not in ready:
            ready.add(pair)
            wide = slice(2 * pair * rank, 2 * (pair + 1) * rank)
            turned = act[:, wide].T
            plain = grad[:, wide]
            for side in range(2):
                columns = slice(side * rank, (side + 1) * rank)
                to = slots[2 * pair + side]
                packed[to, :rank, :] = turned[columns, :]
                packed[to, rank : rank + half, :] = jnp.concatenate([plain[:half, columns], plain[half:, columns]], axis=1)
                packed[to, rank + half :, :] = counts
        if (slot + 1) % share == 0:
            block = pl.ds(slot + 1 - share, share)
            departures.append(pltpu.make_async_copy(packed.at[block], out_hbm.at[block], out_sem.at[slot // share]))
            departures[-1].start()
    for copy in departures:
        copy.wait()


def query_kernel(query_ref, left_ref, right_ref, out_ref, turned):
    rank = left_ref.shape[-1]
    tiles, _, lanes = turned.shape
    some = 4
    step = some * rank
    groups = rank // some

    def iota(shape, dim):
        return lax.broadcasted_iota(jnp.int32, shape, dim)

    repeat = jnp.where(iota((step, rank), 0) // some == iota((step, rank), 1), 1.0, 0.0).astype(jnp.bfloat16)
    right = jnp.concatenate([right_ref[0]] * some, axis=1)
    spread = jnp.dot(repeat, right, preferred_element_type=jnp.float32)
    spread = jnp.where(iota((step, step), 0) % some == iota((step, step), 1) // rank, spread, 0.0).astype(jnp.bfloat16)
    wide = 2 * rank
    column = iota((rank, wide), 1)
    chosen = jnp.where(iota((rank, wide), 0) == some * (column // (2 * some)) + column % some, 1.0, 0.0)
    left = left_ref[0].astype(jnp.float32).T.astype(jnp.bfloat16)
    mixed = jnp.dot(left, chosen.astype(jnp.bfloat16), preferred_element_type=jnp.float32)
    second = column // some % 2 == 1
    mixed = jnp.concatenate([jnp.where(second, 0.0, mixed), jnp.where(second, mixed, 0.0)], axis=0).astype(jnp.bfloat16)
    mixed = jnp.concatenate([mixed, mixed], axis=1)
    for tile in range(tiles):
        columns = slice(tile * lanes, (tile + 1) * lanes)
        for t in range(groups):
            turned[tile, t * step : (t + 1) * step, :] = lax.dot_general(
                spread,
                query_ref[columns, t * step : (t + 1) * step],
                (((1,), (1,)), ((), ())),
                preferred_element_type=jnp.float32,
            )
        for pair in range(rank // 2):
            at = pair * 2 * some
            value = jnp.concatenate(
                [turned[tile, t * step + at : t * step + at + 2 * some, :] for t in range(groups)], axis=0
            )
            high = value.astype(jnp.bfloat16)
            low = (value - high.astype(jnp.float32)).astype(jnp.bfloat16)
            product = jnp.dot(mixed, jnp.concatenate([high, low], axis=0), preferred_element_type=jnp.float32)
            out_ref[pair * wide : (pair + 1) * wide, columns] = product.astype(jnp.bfloat16)


def owner_kernel(scale, order, slots, recv, query, out_ref, grads, per_example):
    blocks, height, width = recv.shape
    rank = grads.shape[1]
    rows = width
    half_rows = rows // 2
    examples = height - rank - half_rows
    pairs = rank // 2
    first_half = lax.broadcasted_iota(jnp.int32, (half_rows, width), 1) < rank

    def one(b):
        counts = recv[b, rank + half_rows :, :].astype(jnp.float32)
        slot = b % grads.shape[0]
        grads[slot] = recv[b, :rank, :].astype(jnp.float32)
        acts = recv[b, rank : rank + half_rows, :]
        swapped = jnp.concatenate([acts[:, rank:], acts[:, :rank]], axis=1)
        zero = jnp.zeros_like(acts)
        weights = jnp.concatenate(
            [
                jnp.where(first_half, acts, zero),
                jnp.where(first_half, swapped, zero),
                jnp.where(first_half, zero, swapped),
                jnp.where(first_half, zero, acts),
            ],
            axis=0,
        )
        columns = []
        for parity in range(2):
            pieces = [grads[slot, pl.ds(2 * p + parity, 1), :] * counts for p in range(pairs)]
            columns.append(jnp.concatenate(pieces, axis=0).astype(jnp.bfloat16))
        weighted = jnp.concatenate(columns, axis=1)
        return jnp.dot(weighted, weights, preferred_element_type=jnp.float32) * scale

    for b in range(0, blocks, 2):
        first, second = one(slots[b]), one(slots[b + 1])
        for p in range(pairs):
            piece = slice(p * examples, (p + 1) * examples)
            per_example[b * examples : (b + 2) * examples, p * width : (p + 1) * width] = jnp.concatenate(
                [first[piece], second[piece]], axis=0
            ).astype(jnp.bfloat16)

    scores = jnp.dot(per_example[...], query[...], preferred_element_type=jnp.float32).T
    tile = out_ref.shape[1]
    for slot, member in enumerate(order):
        out_ref[slot] = scores[member * tile : (member + 1) * tile]


def hop_order(chips):
    far = sorted(range(chips // 2, chips), key=lambda k: (k & 1, -k))
    near = list(range(1, chips // 2))
    order = []
    for at, k in enumerate(far):
        order.append(k)
        order.extend(near[at : at + 1])
    return order


def hop_pack_kernel(act_hbm, grad_hbm, tok_hbm, *refs):
    chips = len(refs) - 6
    outs = refs[:chips]
    act, grad, tok, packed, in_sem, out_sem = refs[chips:]
    chip = lax.axis_index("module") // 2
    rows = act.shape[0]
    rank = act.shape[1] // (2 * chips)
    half = rows // 2
    examples, tokens = tok.shape
    tok_copy = pltpu.make_async_copy(tok_hbm, tok, in_sem.at[0])
    grad_copy = pltpu.make_async_copy(grad_hbm, grad, in_sem.at[1])
    act_copy = pltpu.make_async_copy(act_hbm, act, in_sem.at[2])
    tok_copy.start()
    grad_copy.start()
    act_copy.start()

    tok_copy.wait()
    local = tok[...]
    row_of_lane = lax.broadcasted_iota(jnp.int32, (examples, rows), 1)
    counts = jnp.zeros((examples, rows), jnp.float32)
    for t in range(tokens):
        counts += jnp.where(local[:, t : t + 1] == row_of_lane, 1.0, 0.0)
    counts = counts.astype(jnp.bfloat16)

    grad_copy.wait()
    act_copy.wait()
    for other in range(chips):
        wide = slice(2 * other * rank, 2 * (other + 1) * rank)
        turned = act[:, wide].T
        plain = grad[:, wide]
        distance = chip ^ other
        for side in range(2):
            columns = slice(side * rank, (side + 1) * rank)
            packed[distance, side, :rank, :] = turned[columns, :]
            packed[distance, side, rank : rank + half, :] = jnp.concatenate(
                [plain[:half, columns], plain[half:, columns]], axis=1
            )
            packed[distance, side, rank + half :, :] = counts
    departures = [pltpu.make_async_copy(packed.at[k], outs[k], out_sem.at[k]) for k in range(chips)]
    for copy in departures:
        copy.start()
    for copy in departures:
        copy.wait()


def hop_owner_kernel(scale, order, *refs):
    chips = len(refs) - 6
    arrived = refs[:chips]
    own_query, other_query, out_ref, grads, per_example, placed = refs[chips:]
    core = lax.axis_index("module") % 2
    chip = lax.axis_index("module") // 2
    _, height, width = arrived[0].shape
    rank = grads.shape[1]
    half_rows = width // 2
    examples = height - rank - half_rows
    pairs = rank // 2
    first_half = lax.broadcasted_iota(jnp.int32, (half_rows, width), 1) < rank

    def one(block, side, slot):
        counts = block[side, rank + half_rows :, :].astype(jnp.float32)
        grads[slot] = block[side, :rank, :].astype(jnp.float32)
        acts = block[side, rank : rank + half_rows, :]
        swapped = jnp.concatenate([acts[:, rank:], acts[:, :rank]], axis=1)
        zero = jnp.zeros_like(acts)
        weights = jnp.concatenate(
            [
                jnp.where(first_half, acts, zero),
                jnp.where(first_half, swapped, zero),
                jnp.where(first_half, zero, swapped),
                jnp.where(first_half, zero, acts),
            ],
            axis=0,
        )
        columns = []
        for parity in range(2):
            pieces = [grads[slot, pl.ds(2 * p + parity, 1), :] * counts for p in range(pairs)]
            columns.append(jnp.concatenate(pieces, axis=0).astype(jnp.bfloat16))
        weighted = jnp.concatenate(columns, axis=1)
        return jnp.dot(weighted, weights, preferred_element_type=jnp.float32) * scale

    scores = []
    for turn, query in enumerate((own_query, other_query)):
        side = core if turn == 0 else 1 - core
        for k in range(0, chips, 2):
            slot = (turn * chips + k) % grads.shape[0]
            first, second = one(arrived[k], side, slot), one(arrived[k + 1], side, slot + 1)
            for p in range(pairs):
                piece = slice(p * examples, (p + 1) * examples)
                per_example[turn, k * examples : (k + 2) * examples, p * width : (p + 1) * width] = jnp.concatenate(
                    [first[piece], second[piece]], axis=0
                ).astype(jnp.bfloat16)
        scores.append(jnp.dot(per_example[turn], query[...], preferred_element_type=jnp.float32))
    total = scores[0] + scores[1]
    placed[...] = jnp.zeros_like(placed)
    for k in range(chips):
        block = 2 * (chip ^ k) + core
        placed[pl.ds(pl.multiple_of(block * examples, examples), examples), :] = total[k * examples : (k + 1) * examples]
    turned = placed[...].T
    tile = out_ref.shape[1]
    for slot, member in enumerate(order):
        out_ref[slot] = turned[member * tile : (member + 1) * tile]


def per_device(owners, act_table, grad_table, token_rows, left_inv, right_inv, query_grads):
    rows, columns = act_table.shape
    examples, tokens = token_rows.shape
    local_modules, rank, _ = left_inv.shape
    queries = query_grads.shape[0]
    width = 2 * rank
    lanes = min(queries, 128)
    assert queries % lanes == 0
    assert local_modules == 1 and columns == owners * rank and owners % 4 == 0
    assert rows == width and tokens <= 256 and examples % 8 == 0
    height = rank + rows // 2 + examples
    chips = owners // 2
    scale = 1.0 / math.sqrt(tokens)
    back = member_order(owners, owners * FIRST_BACK // 16)
    limit = pltpu.CompilerParams(vmem_limit_bytes=VMEM_LIMIT)
    partial_shape = jax.ShapeDtypeStruct((owners, queries // owners, owners * examples), jnp.float32)
    tables = [
        pltpu.VMEM((rows, columns), jnp.bfloat16),
        pltpu.VMEM((rows, columns), jnp.bfloat16),
        pltpu.VMEM((examples, tokens), jnp.int32),
    ]

    def exchange(pieces, order):
        return lax.all_to_all(
            pieces, "module", split_axis=0, concat_axis=0, axis_index_groups=[order], tiled=True
        )

    def prepare():
        return pl.pallas_call(
            query_kernel,
            out_shape=jax.ShapeDtypeStruct((rank * rank, queries), jnp.bfloat16),
            scratch_shapes=[
                pltpu.VMEM((queries // lanes, rank * rank, lanes), jnp.float32),
            ],
            cost_estimate=pl.CostEstimate(
                flops=4 * queries * rank**3, bytes_accessed=4 * queries * rank**2, transcendentals=0
            ),
            compiler_params=limit,
            name="prepare",
        )(query_grads.reshape(queries, rank * rank), left_inv, right_inv)

    def by_exchange():
        order = member_order(owners, owners * FIRST_OUT // 16)
        slots = [order.index(member) for member in range(owners)]
        packed = pl.pallas_call(
            functools.partial(pack_kernel, slots),
            out_shape=jax.ShapeDtypeStruct((owners, height, width), jnp.bfloat16),
            in_specs=[pl.BlockSpec(memory_space=pltpu.HBM)] * 3,
            out_specs=pl.BlockSpec(memory_space=pltpu.HBM),
            scratch_shapes=tables
            + [
                pltpu.VMEM((owners, height, width), jnp.bfloat16),
                pltpu.SemaphoreType.DMA((3,)),
                pltpu.SemaphoreType.DMA((2,)),
            ],
            name="pack",
        )(act_table, grad_table, token_rows)
        recv = exchange(packed, order)
        return pl.pallas_call(
            functools.partial(owner_kernel, scale, back, slots),
            out_shape=partial_shape,
            scratch_shapes=[
                pltpu.VMEM((4, rank, rows), jnp.float32),
                pltpu.VMEM((owners * examples, rank * rank), jnp.bfloat16),
            ],
            compiler_params=limit,
            name="owner",
        )(recv, prepare())

    def by_hops():
        packed = pl.pallas_call(
            hop_pack_kernel,
            out_shape=[jax.ShapeDtypeStruct((2, height, width), jnp.bfloat16)] * chips,
            in_specs=[pl.BlockSpec(memory_space=pltpu.HBM)] * 3,
            out_specs=[pl.BlockSpec(memory_space=pltpu.HBM)] * chips,
            scratch_shapes=tables
            + [
                pltpu.VMEM((chips, 2, height, width), jnp.bfloat16),
                pltpu.SemaphoreType.DMA((3,)),
                pltpu.SemaphoreType.DMA((chips,)),
            ],
            name="pack",
        )(act_table, grad_table, token_rows)
        arrived = list(packed)
        for k in hop_order(chips):
            arrived[k] = lax.ppermute(packed[k], "module", [(i, i ^ (2 * k)) for i in range(owners)])
        prepared = prepare()
        swapped = lax.ppermute(prepared, "module", [(i, i ^ 1) for i in range(owners)])
        return pl.pallas_call(
            functools.partial(hop_owner_kernel, scale, back),
            out_shape=partial_shape,
            scratch_shapes=[
                pltpu.VMEM((4, rank, rows), jnp.float32),
                pltpu.VMEM((2, chips * examples, rank * rank), jnp.bfloat16),
                pltpu.VMEM((owners * examples, queries), jnp.float32),
            ],
            compiler_params=limit,
            name="owner",
        )(*arrived, prepared, swapped)

    partial = by_hops() if hopping(owners) else by_exchange()
    return jnp.sum(exchange(partial, back), axis=0)


def hopping(owners):
    return owners & (owners - 1) == 0 and owners <= MOST_HOPPING


def solution(mesh):
    placed = (
        P(("groups", "module"), None),
        P(("groups", "module"), None),
        P(("groups", "module"), None),
        P("module", None, None),
        P("module", None, None),
        P("groups", "module", None),
    )
    owners = mesh.shape["module"]
    return jax.shard_map(
        functools.partial(per_device, owners),
        mesh=mesh,
        in_specs=placed,
        out_specs=P(("groups", "module"), None),
        check_vma=False,
    )
```

time: 33.5 us -> 39 us (1.16)
  starting transfers between devices: 7.62 us -> 14.2 us
  local copies, waits for them, and re-layouts: 0.02 us -> 3.54 us
  Pallas kernels: 6.51 us -> 4.92 us
  blocking collectives: 11.2 us -> 9.62 us
  waiting for transfers between devices: 7.22 us -> 5.69 us
    ppermute x0 -> x8, starting transfers between devices: none -> 14.2 us  [the longest x7 13.7 us: by_hops(): lax.ppermute(packed[k], 'module', [(i, i ^ 2 * k) for i in range(owners)])]
    all_to_all x1 -> x0, starting transfers between devices: 7.62 us -> none  [exchange(): lax.all_to_all(pieces, 'module', split_axis=0, concat_axis=0, axis_index_...]
    all_to_all x1 -> x0, waiting for transfers between devices: 7.22 us -> none  [exchange(): lax.all_to_all(pieces, 'module', split_axis=0, concat_axis=0, axis_index_...]
    ppermute x0 -> x8, waiting for transfers between devices: none -> 5.69 us  [the longest x7 5.69 us: by_hops(): lax.ppermute(packed[k], 'module', [(i, i ^ 2 * k) for i in range(owners)])]
    unnamed x6 -> x8, local copies, waits for them, and re-layouts: 0.02 us -> 3.54 us
    pallas_call x3, Pallas kernels: 6.51 us -> 4.92 us  [the longest x1 2.15 us: by_hops(): pl.pallas_call(hop_pack_kernel, out_shape=[jax.ShapeDtypeStruct((2, heigh...]
    all_to_all x1, blocking collectives: 11.2 us -> 9.62 us  [exchange(): lax.all_to_all(pieces, 'module', split_axis=0, concat_axis=0, axis_index_...]
  transfers between devices with their start and end apart: 1 -> 8, of which waited for: 1 -> 2; matrix products, arithmetic and copies ran while one was open for 0% -> 0% of each run, Pallas kernels for 10% -> 6%
where the time goes in v5:
time: 39 us; the launch traced here: 38.6 us
  starting transfers between devices  14.2 us (36%)
  blocking collectives  9.62 us (25%)
  waiting for transfers between devices  5.69 us (15%)
  Pallas kernels  4.92 us (13%)
  local copies, waits for them, and re-layouts  3.54 us (9%)
  other arithmetic  0.61 us (2%)
    ppermute x7, starting transfers between devices, by_hops(): lax.ppermute(packed[k], 'module', [(i, i ^ 2 * k) for i in range(owners)])  13.7 us
    all_to_all x1, blocking collectives, exchange(): lax.all_to_all(pieces, 'module', split_axis=0, concat_axis=0, axis_index_...  9.62 us
    ppermute x7, waiting for transfers between devices, by_hops(): lax.ppermute(packed[k], 'module', [(i, i ^ 2 * k) for i in range(owners)])  5.69 us
    unnamed x8, local copies, waits for them, and re-layouts  3.54 us
    pallas_call x1, Pallas kernels, by_hops(): pl.pallas_call(hop_pack_kernel, out_shape=[jax.ShapeDtypeStruct((2, heigh...  2.15 us
    pallas_call x1, Pallas kernels, prepare(): pl.pallas_call(query_kernel, out_shape=jax.ShapeDtypeStruct((rank * rank,...  1.49 us
    pallas_call x1, Pallas kernels, by_hops(): pl.pallas_call(functools.partial(hop_owner_kernel, scale, back), out_shap...  1.27 us
  transfers between devices with their start and end apart: 8, of which 2 were waited for; matrix products, arithmetic and copies ran while one was open for 0% of the time, Pallas kernels for 6%

profile of v5, /device:TPU:0, one launch (start us, length us, event | category | flops | bytes accessed | tf_op | source)
XLA Modules:
  0.0 38.6 jit_solution(10489335646958578894)
XLA Ops:
  0.0 0.0 copy-start
  0.0 1.2 %copy-done = bf16[128,1,4096]{2,0,1:T(8,128)(2,1)S(1)} copy-done((bf16[128,1,4096]{2,0,1:T(8,128)(2,1)S(1)}, bf16[128,1,4096]{2,0,1:T(8,128)(2,1)}, u32[]{:S(2)}) %copy-start) | copy-done | bytes 1048600
  1.2 0.0 copy-start.2
  1.2 0.7 %copy-done.2 = bf16[1,64,64]{2,1,0:T(8,128)(2,1)S(1)} copy-done((bf16[1,64,64]{2,1,0:T(8,128)(2,1)S(1)}, bf16[1,64,64]{2,1,0:T(8,128)(2,1)}, u32[]{:S(2)}) %copy-start.2) | copy-done | bytes 8216
  1.9 0.0 copy-start.3
  1.9 0.7 %copy-done.3 = bf16[1,64,64]{2,1,0:T(8,128)(2,1)S(1)} copy-done((bf16[1,64,64]{2,1,0:T(8,128)(2,1)S(1)}, bf16[1,64,64]{2,1,0:T(8,128)(2,1)}, u32[]{:S(2)}) %copy-start.3) | copy-done | bytes 8216
  2.7 1.5 %prepare.1.refs_8_ = bf16[4096,128]{1,0:T(8,128)(2,1)S(1)} custom-call(bf16[128,4096]{1,0:T(8,128)(2,1)S(1)} %bitcast.1, bf16[1,64,64]{2,1,0:T(8,128)(2,1)S(1)} %copy-done.2, bf16[1,64,64]{2,1,0:T(8,128)(2,1)S(1)} %copy-done.3), custom_call_target="tpu_custom_call" | custom-call | flops 134217728 | bytes 2097152 | tf_op jit(solution)/shard_map/prepare/pallas_call | solution.py:300
  4.2 0.6 %collective-permute-start.7 = (bf16[4096,128]{1,0:T(8,128)(2,1)S(1)}, bf16[4096,128]{1,0:T(8,128)(2,1)S(1)}, u32[]{:S(2)}, u32[]{:S(2)}) collective-permute-start(bf16[4096,128]{1,0:T(8,128)(2,1)S(1)} %prepare.1.refs_8_), channel_id=1, source_target_pairs={{0,1},{1,0},{2,3},{3,2},{4,5},{5,4},{6,7},{7,6},{8,9},{9,8},{10,11... | collective-permute-start | bytes 3145736 | tf_op jit(solution)/shard_map/ppermute | solution.py:359
  4.7 2.2 %pack.1 = (bf16[2,136,128]{2,1,0:T(8,128)(2,1)}, bf16[2,136,128]{2,1,0:T(8,128)(2,1)}, bf16[2,136,128]{2,1,0:T(8,128)(2,1)}, bf16[2,136,128]{2,1,0:T(8,128)(2,1)...) custom-call(bf16[128,1024]{1,0:T(8,128)(2,1)} %act_hbm.1, ...), custom_call_target="tpu_custom_call" | custom-call | tf_op jit(solution)/shard_map/pack/pallas_call | solution.py:342
  6.9 2.6 %collective-permute-start = (bf16[2,136,128]{2,1,0:T(8,128)(2,1)}, bf16[2,136,128]{2,1,0:T(8,128)(2,1)S(1)}, u32[]{:S(2)}, u32[]{:S(2)}) collective-permute-start(bf16[2,136,128]{2,1,0:T(8,128)(2,1)} %get-tuple-element.14), channel_id=1, source_target_pairs={{0,2},{1,3},{2,0},{3,1},{4,6},{5,7},{6,4},{7,5},{8,10},{9,11},{10,... | collective-permute-start | bytes 208904 | tf_op jit(solution)/shard_map/ppermute | solution.py:357
  9.5 1.6 %collective-permute-start.1 = (bf16[2,136,128]{2,1,0:T(8,128)(2,1)}, bf16[2,136,128]{2,1,0:T(8,128)(2,1)S(1)}, u32[]{:S(2)}, u32[]{:S(2)}) collective-permute-start(bf16[2,136,128]{2,1,0:T(8,128)(2,1)} %get-tuple-element.15), channel_id=1, source_target_pairs={{0,4},{1,5},{2,6},{3,7},{4,0},{5,1},{6,2},{7,3},{8,12},{9,13},{10,... | collective-permute-start | bytes 208904 | tf_op jit(solution)/shard_map/ppermute | solution.py:357
  11.0 0.0 collective-permute-start.2
  11.0 3.0 %collective-permute-start.3 = (bf16[2,136,128]{2,1,0:T(8,128)(2,1)}, bf16[2,136,128]{2,1,0:T(8,128)(2,1)S(1)}, u32[]{:S(2)}, u32[]{:S(2)}) collective-permute-start(bf16[2,136,128]{2,1,0:T(8,128)(2,1)} %get-tuple-element.17), channel_id=1, source_target_pairs={{0,8},{1,9},{2,10},{3,11},{4,12},{5,13},{6,14},{7,15},{8,0},{9,1},... | collective-permute-start | bytes 208904 | tf_op jit(solution)/shard_map/ppermute | solution.py:357
  14.0 0.0 collective-permute-done.refs_1_
  14.0 2.2 %collective-permute-start.4 = (bf16[2,136,128]{2,1,0:T(8,128)(2,1)}, bf16[2,136,128]{2,1,0:T(8,128)(2,1)S(1)}, u32[]{:S(2)}, u32[]{:S(2)}) collective-permute-start(bf16[2,136,128]{2,1,0:T(8,128)(2,1)} %get-tuple-element.18), channel_id=1, source_target_pairs={{0,10},{1,11},{2,8},{3,9},{4,14},{5,15},{6,12},{7,13},{8,2},{9,3},... | collective-permute-start | bytes 208904 | tf_op jit(solution)/shard_map/ppermute | solution.py:357
  16.3 0.0 collective-permute-done.1.refs_2_
  16.3 2.6 %collective-permute-start.5 = (bf16[2,136,128]{2,1,0:T(8,128)(2,1)}, bf16[2,136,128]{2,1,0:T(8,128)(2,1)S(1)}, u32[]{:S(2)}, u32[]{:S(2)}) collective-permute-start(bf16[2,136,128]{2,1,0:T(8,128)(2,1)} %get-tuple-element.19), channel_id=1, source_target_pairs={{0,12},{1,13},{2,14},{3,15},{4,8},{5,9},{6,10},{7,11},{8,4},{9,5},... | collective-permute-start | bytes 208904 | tf_op jit(solution)/shard_map/ppermute | solution.py:357
  18.9 0.0 collective-permute-done.2.refs_3_
  18.9 1.6 %collective-permute-start.6 = (bf16[2,136,128]{2,1,0:T(8,128)(2,1)}, bf16[2,136,128]{2,1,0:T(8,128)(2,1)S(1)}, u32[]{:S(2)}, u32[]{:S(2)}) collective-permute-start(bf16[2,136,128]{2,1,0:T(8,128)(2,1)} %get-tuple-element.20), channel_id=1, source_target_pairs={{0,14},{1,15},{2,12},{3,13},{4,10},{5,11},{6,8},{7,9},{8,6},{9,7},... | collective-permute-start | bytes 208904 | tf_op jit(solution)/shard_map/ppermute | solution.py:357
  20.6 0.0 collective-permute-done.3.refs_4_
  20.6 4.3 %collective-permute-done.4.refs_5_ = bf16[2,136,128]{2,1,0:T(8,128)(2,1)S(1)} collective-permute-done((bf16[2,136,128]{2,1,0:T(8,128)(2,1)}, bf16[2,136,128]{2,1,0:T(8,128)(2,1)S(1)}, u32[]{:S(2)}, u32[]{:S(2)}) %collective-permute-start.4) | collective-permute-done | bytes 69664 | tf_op jit(solution)/shard_map/ppermute | solution.py:357
  24.9 0.0 collective-permute-done.5.refs_6_
  24.9 1.3 %collective-permute-done.6.refs_7_ = bf16[2,136,128]{2,1,0:T(8,128)(2,1)S(1)} collective-permute-done((bf16[2,136,128]{2,1,0:T(8,128)(2,1)}, bf16[2,136,128]{2,1,0:T(8,128)(2,1)S(1)}, u32[]{:S(2)}, u32[]{:S(2)}) %collective-permute-start.6) | collective-permute-done | bytes 69664 | tf_op jit(solution)/shard_map/ppermute | solution.py:357
  26.3 0.0 collective-permute-done.7.refs_9_
  26.3 0.0 copy-start.1
  26.3 0.9 %copy-done.1 = bf16[2,136,128]{2,1,0:T(8,128)(2,1)S(1)} copy-done((bf16[2,136,128]{2,1,0:T(8,128)(2,1)S(1)}, bf16[2,136,128]{2,1,0:T(8,128)(2,1)}, u32[]{:S(2)}) %copy-start.1) | copy-done | bytes 69656
  27.1 1.3 %owner.1 = f32[16,8,128]{2,1,0:T(8,128)S(1)} custom-call(bf16[2,136,128]{2,1,0:T(8,128)(2,1)S(1)} %copy-done.1, bf16[2,136,128]{2,1,0:T(8,128)(2,1)S(1)} %collective-permute-done.refs_1_, bf16[2,136,128]{2,1,0:T(8,128)(2,1)S(1)} %collective-permute-done.1.refs_2_, bf16[2,136,128]{2,1,0:T(8,128)(2,1)S(1)} %collective-permute-done.2.refs_3_, ...), custom_call_target="tpu_custom_call" | custom-call | tf_op jit(solution)/shard_map/owner/pallas_call | solution.py:360
  28.4 9.6 %all_to_all.5 = f32[16,8,128]{2,1,0:T(8,128)S(1)} all-to-all(f32[16,8,128]{2,1,0:T(8,128)S(1)} %owner.1), channel_id=1, replica_groups={{11,0,1,2,3,4,5,12,13,6,7,8,9,14,15,10},{27,16,17,18,19,20,21,28,29,22,..., dimensions={0} | all-to-all | bytes 131072 | tf_op jit(solution)/shard_map/all_to_all | solution.py:295
  38.0 0.6 %reduce_sum.9 = f32[8,128]{1,0:T(8,128)} reduce(f32[16,8,128]{2,1,0:T(8,128)S(1)} %all_to_all.5, f32[]{:T(128)} %constant.0.clone.1), dimensions={0}, to_apply=%region_0.0 | reduce | flops 15360 | bytes 69636 | tf_op jit(solution)/shard_map/reduce_sum | solution.py:373
Async XLA Ops:
  0.0 1.2 %copy-start = (bf16[128,1,4096]{2,0,1:T(8,128)(2,1)S(1)}, bf16[128,1,4096]{2,0,1:T(8,128)(2,1)}, u32[]{:S(2)}) copy-start(bf16[128,1,4096]{2,0,1:T(8,128)(2,1)} %param.11) | copy-start | bytes 3145732
  1.2 0.7 %copy-start.2 = (bf16[1,64,64]{2,1,0:T(8,128)(2,1)S(1)}, bf16[1,64,64]{2,1,0:T(8,128)(2,1)}, u32[]{:S(2)}) copy-start(bf16[1,64,64]{2,1,0:T(8,128)(2,1)} %left_ref.1) | copy-start | bytes 24580
  1.9 0.7 %copy-start.3 = (bf16[1,64,64]{2,1,0:T(8,128)(2,1)S(1)}, bf16[1,64,64]{2,1,0:T(8,128)(2,1)}, u32[]{:S(2)}) copy-start(bf16[1,64,64]{2,1,0:T(8,128)(2,1)} %right_ref.1) | copy-start | bytes 24580
  4.2 22.1 %collective-permute-start.7 = (bf16[4096,128]{1,0:T(8,128)(2,1)S(1)}, bf16[4096,128]{1,0:T(8,128)(2,1)S(1)}, u32[]{:S(2)}, u32[]{:S(2)}) collective-permute-start(bf16[4096,128]{1,0:T(8,128)(2,1)S(1)} %prepare.1.refs_8_), channel_id=1, source_target_pairs={{0,1},{1,0},{2,3},{3,2},{4,5},{5,4},{6,7},{7,6},{8,9},{9,8},{10,11... | collective-permute-start | bytes 3145736 | tf_op jit(solution)/shard_map/ppermute | solution.py:359
  6.9 7.1 %collective-permute-start = (bf16[2,136,128]{2,1,0:T(8,128)(2,1)}, bf16[2,136,128]{2,1,0:T(8,128)(2,1)S(1)}, u32[]{:S(2)}, u32[]{:S(2)}) collective-permute-start(bf16[2,136,128]{2,1,0:T(8,128)(2,1)} %get-tuple-element.14), channel_id=1, source_target_pairs={{0,2},{1,3},{2,0},{3,1},{4,6},{5,7},{6,4},{7,5},{8,10},{9,11},{10,... | collective-permute-start | bytes 208904 | tf_op jit(solution)/shard_map/ppermute | solution.py:357
  9.5 6.8 %collective-permute-start.1 = (bf16[2,136,128]{2,1,0:T(8,128)(2,1)}, bf16[2,136,128]{2,1,0:T(8,128)(2,1)S(1)}, u32[]{:S(2)}, u32[]{:S(2)}) collective-permute-start(bf16[2,136,128]{2,1,0:T(8,128)(2,1)} %get-tuple-element.15), channel_id=1, source_target_pairs={{0,4},{1,5},{2,6},{3,7},{4,0},{5,1},{6,2},{7,3},{8,12},{9,13},{10,... | collective-permute-start | bytes 208904 | tf_op jit(solution)/shard_map/ppermute | solution.py:357
  11.0 7.9 %collective-permute-start.2 = (bf16[2,136,128]{2,1,0:T(8,128)(2,1)}, bf16[2,136,128]{2,1,0:T(8,128)(2,1)S(1)}, u32[]{:S(2)}, u32[]{:S(2)}) collective-permute-start(bf16[2,136,128]{2,1,0:T(8,128)(2,1)} %get-tuple-element.16), channel_id=1, source_target_pairs={{0,6},{1,7},{2,4},{3,5},{4,2},{5,3},{6,0},{7,1},{8,14},{9,15},{10,... | collective-permute-start | bytes 208904 | tf_op jit(solution)/shard_map/ppermute | solution.py:357
  11.0 9.5 %collective-permute-start.3 = (bf16[2,136,128]{2,1,0:T(8,128)(2,1)}, bf16[2,136,128]{2,1,0:T(8,128)(2,1)S(1)}, u32[]{:S(2)}, u32[]{:S(2)}) collective-permute-start(bf16[2,136,128]{2,1,0:T(8,128)(2,1)} %get-tuple-element.17), channel_id=1, source_target_pairs={{0,8},{1,9},{2,10},{3,11},{4,12},{5,13},{6,14},{7,15},{8,0},{9,1},... | collective-permute-start | bytes 208904 | tf_op jit(solution)/shard_map/ppermute | solution.py:357
  14.0 10.9 %collective-permute-start.4 = (bf16[2,136,128]{2,1,0:T(8,128)(2,1)}, bf16[2,136,128]{2,1,0:T(8,128)(2,1)S(1)}, u32[]{:S(2)}, u32[]{:S(2)}) collective-permute-start(bf16[2,136,128]{2,1,0:T(8,128)(2,1)} %get-tuple-element.18), channel_id=1, source_target_pairs={{0,10},{1,11},{2,8},{3,9},{4,14},{5,15},{6,12},{7,13},{8,2},{9,3},... | collective-permute-start | bytes 208904 | tf_op jit(solution)/shard_map/ppermute | solution.py:357
  16.3 8.6 %collective-permute-start.5 = (bf16[2,136,128]{2,1,0:T(8,128)(2,1)}, bf16[2,136,128]{2,1,0:T(8,128)(2,1)S(1)}, u32[]{:S(2)}, u32[]{:S(2)}) collective-permute-start(bf16[2,136,128]{2,1,0:T(8,128)(2,1)} %get-tuple-element.19), channel_id=1, source_target_pairs={{0,12},{1,13},{2,14},{3,15},{4,8},{5,9},{6,10},{7,11},{8,4},{9,5},... | collective-permute-start | bytes 208904 | tf_op jit(solution)/shard_map/ppermute | solution.py:357
  18.9 7.3 %collective-permute-start.6 = (bf16[2,136,128]{2,1,0:T(8,128)(2,1)}, bf16[2,136,128]{2,1,0:T(8,128)(2,1)S(1)}, u32[]{:S(2)}, u32[]{:S(2)}) collective-permute-start(bf16[2,136,128]{2,1,0:T(8,128)(2,1)} %get-tuple-element.20), channel_id=1, source_target_pairs={{0,14},{1,15},{2,12},{3,13},{4,10},{5,11},{6,8},{7,9},{8,6},{9,7},... | collective-permute-start | bytes 208904 | tf_op jit(solution)/shard_map/ppermute | solution.py:357
  26.3 0.9 %copy-start.1 = (bf16[2,136,128]{2,1,0:T(8,128)(2,1)S(1)}, bf16[2,136,128]{2,1,0:T(8,128)(2,1)}, u32[]{:S(2)}) copy-start(bf16[2,136,128]{2,1,0:T(8,128)(2,1)} %get-tuple-element.13.refs_0_) | copy-start | bytes 208900
